TPU v7x, 128 devices: a whole 4x4x4 slice. The times are simulated.
128 devices in a mesh: dp: 4 (over z_lo, core), mp: 32 (over y, z_hi, x).
Axes of the slice: x: 4, y: 4, z: 4 (z_hi: 2, z_lo: 2; z = z_hi * 2 + z_lo), core: 2. Of those that a mesh axis runs over, the one named last changes fastest.
Arguments:
- fields: float32 [4, 32, 128, 128, 128], P('dp', None, 'mp'), may hold values from -6 to 6
- upstream: bfloat16 [4, 32, 128, 128, 128], P('dp', None, 'mp'), may hold values from -6 to 6
- spectral_weight: float32 [2, 32, 32, 32, 1024], P(None, None, None, 'dp', 'mp'), may hold values from -4.2 to 4.2
- point_weight: float32 [32, 32], replicated, may hold values from -1 to 1
- point_bias: float32 [32], replicated, may hold values from -3 to 3
Outputs:
- grad_fields: float32 [4, 32, 128, 128, 128], P('dp', None, 'mp')
- grad_weight: float32 [2, 32, 32, 32, 1024], P(None, None, None, 'dp', 'mp')
All inputs are finite; a program needn't handle non-finite values.
Results may differ from a plain program's by a relative error of at most 0.0003.
Values sent between devices are 32-bit elements; how exact they have to be, the bound alone decides.
A program may use at most 256 MiB of HBM per device.

v0:
```python
from functools import partial
import math

import jax
import jax.numpy as jnp
from jax import lax
from jax.sharding import PartitionSpec as P

NX = 128
NY = 128
NZ = 128
MX = 32
MY = 32
MZ = 32


HIGHEST = lax.Precision.HIGHEST


def tables(number, kept_modes, signed):
    positions = jnp.arange(number, dtype=jnp.int32)
    frequency = jnp.arange(kept_modes, dtype=jnp.int32)
    if signed:
        frequency = jnp.where(frequency < kept_modes // 2, frequency, frequency - kept_modes)
    phases = jnp.mod(positions[:, None] * frequency[None, :], number).astype(jnp.float32) * (
        2.0 * math.pi / number
    )
    return jnp.concatenate([jnp.cos(phases), jnp.sin(phases)], axis=1)


def forward_plane(grid_field, table_y, table_z):
    along_y = jnp.einsum("scpyz,yj->scpjz", grid_field, table_y, precision=HIGHEST)
    products = jnp.einsum("scpjz,zk->scpjk", along_y, table_z, precision=HIGHEST)
    cos_cos = products[:, :, :, :MY, :MZ]
    cos_sin = products[:, :, :, :MY, MZ:]
    sin_cos = products[:, :, :, MY:, :MZ]
    sin_sin = products[:, :, :, MY:, MZ:]
    result = jnp.stack([cos_cos - sin_sin, -(sin_cos + cos_sin)], axis=3)
    return result.reshape(result.shape[:4] + (MY * MZ,))


def forward_line(pieces, table_x):
    products = jnp.einsum("scxrm,xk->scrkm", pieces, table_x, precision=HIGHEST)
    real_part = products[:, :, 0, :MX] + products[:, :, 1, MX:]
    imag_part = products[:, :, 1, :MX] - products[:, :, 0, MX:]
    return jnp.stack([real_part, imag_part], axis=2)


def inverse_line(spectrum, table_x):
    real_part = spectrum[:, :, 0]
    imag_part = spectrum[:, :, 1]
    stacked = jnp.stack(
        [
            jnp.concatenate([real_part, -imag_part], axis=2),
            jnp.concatenate([imag_part, real_part], axis=2),
        ],
        axis=2,
    )
    return jnp.einsum("scrjm,xj->scxrm", stacked, table_x, precision=HIGHEST)


def inverse_plane(pieces, table_y, table_z):
    shaped = pieces.reshape(pieces.shape[:4] + (MY, MZ))
    real_part = shaped[:, :, :, 0]
    imag_part = shaped[:, :, :, 1]
    stacked = jnp.stack(
        [
            jnp.concatenate([real_part, -imag_part], axis=3),
            jnp.concatenate([imag_part, real_part], axis=3),
        ],
        axis=3,
    )
    along_y = jnp.einsum("scpwjk,yj->scpwyk", stacked, table_y, precision=HIGHEST)
    merged = jnp.concatenate([along_y[:, :, :, 0], -along_y[:, :, :, 1]], axis=4)
    return jnp.einsum("scpyj,zj->scpyz", merged, table_z, precision=HIGHEST)


def mix_forward(weight, spectrum):
    real_weight = weight[0]
    imag_weight = weight[1]
    real_spec = spectrum[:, :, 0]
    imag_spec = spectrum[:, :, 1]
    real_part = jnp.einsum(
        "sixm,ioxm->soxm", real_spec, real_weight, precision=HIGHEST
    ) - jnp.einsum("sixm,ioxm->soxm", imag_spec, imag_weight, precision=HIGHEST)
    imag_part = jnp.einsum(
        "sixm,ioxm->soxm", imag_spec, real_weight, precision=HIGHEST
    ) + jnp.einsum("sixm,ioxm->soxm", real_spec, imag_weight, precision=HIGHEST)
    return jnp.stack([real_part, imag_part], axis=2)


def mix_adjoint(weight, gradient):
    real_weight = weight[0]
    imag_weight = weight[1]
    real_grad = gradient[:, :, 0]
    imag_grad = gradient[:, :, 1]
    real_part = jnp.einsum(
        "soxm,ioxm->sixm", real_grad, real_weight, precision=HIGHEST
    ) + jnp.einsum("soxm,ioxm->sixm", imag_grad, imag_weight, precision=HIGHEST)
    imag_part = jnp.einsum(
        "soxm,ioxm->sixm", imag_grad, real_weight, precision=HIGHEST
    ) - jnp.einsum("soxm,ioxm->sixm", real_grad, imag_weight, precision=HIGHEST)
    return jnp.stack([real_part, imag_part], axis=2)


def weight_gradient(gradient, spectrum):
    real_grad = gradient[:, :, 0]
    imag_grad = gradient[:, :, 1]
    real_spec = spectrum[:, :, 0]
    imag_spec = spectrum[:, :, 1]
    real_part = jnp.einsum("soxm,sixm->ioxm", real_grad, real_spec, precision=HIGHEST) + jnp.einsum(
        "soxm,sixm->ioxm", imag_grad, imag_spec, precision=HIGHEST
    )
    imag_part = jnp.einsum("soxm,sixm->ioxm", imag_grad, real_spec, precision=HIGHEST) - jnp.einsum(
        "soxm,sixm->ioxm", real_grad, imag_spec, precision=HIGHEST
    )
    return jnp.stack([real_part, imag_part], axis=0)


def shards(fields, upstream, spectral_weight, point_weight, point_bias):
    table_y = tables(NY, MY, True)
    table_z = tables(NZ, MZ, False)
    table_x = tables(NX, MX, True)
    modes_dev = spectral_weight.shape[4]
    mode_index = lax.axis_index("mp") * modes_dev + jnp.arange(modes_dev, dtype=jnp.int32)
    kz_index = jnp.mod(mode_index, MZ)
    factor = jnp.where(kz_index == 0, 1.0, 2.0).astype(jnp.float32) / float(NX * NY * NZ)

    def to_modes(pieces):
        return forward_line(pieces, table_x)

    def to_cells(pieces):
        return inverse_plane(pieces, table_y, table_z)

    spectrum = to_modes(
        lax.all_to_all(
            forward_plane(fields, table_y, table_z), "mp", split_axis=4, concat_axis=2, tiled=True
        )
    )
    full_weight = lax.all_gather(spectral_weight, "dp", axis=3, tiled=True)
    mixed_spec = mix_forward(full_weight, spectrum)
    mixed_spec = mixed_spec * factor
    spectral_part = to_cells(
        lax.all_to_all(
            inverse_line(mixed_spec, table_x), "mp", split_axis=2, concat_axis=4, tiled=True
        )
    )
    preact = spectral_part + jnp.einsum("scpyz,co->sopyz", fields, point_weight, precision=HIGHEST)
    preact = preact + point_bias[None, :, None, None, None]
    activation, pullback = jax.vjp(partial(jax.nn.gelu, approximate=False), preact)
    grad_pre = pullback(upstream.astype(jnp.float32))[0]
    grad_spec = to_modes(
        lax.all_to_all(
            forward_plane(grad_pre, table_y, table_z), "mp", split_axis=4, concat_axis=2, tiled=True
        )
    )
    grad_spec = grad_spec * factor
    back_spec = mix_adjoint(full_weight, grad_spec)
    weight_out = lax.psum_scatter(
        weight_gradient(grad_spec, spectrum), "dp", scatter_dimension=3, tiled=True
    )
    spectral_back = to_cells(
        lax.all_to_all(
            inverse_line(back_spec, table_x), "mp", split_axis=2, concat_axis=4, tiled=True
        )
    )
    grad_fields = spectral_back + jnp.einsum(
        "sopyz,co->scpyz", grad_pre, point_weight, precision=HIGHEST
    )
    return (grad_fields, weight_out)


def solution(mesh):
    placed = (
        P("dp", None, "mp", None, None),
        P("dp", None, "mp", None, None),
        P(None, None, None, "dp", "mp"),
        P(),
        P(),
    )
    return jax.shard_map(
        shards,
        mesh=mesh,
        in_specs=placed,
        out_specs=(P("dp", None, "mp", None, None), P(None, None, None, "dp", "mp")),
        check_vma=False,
    )
```

profile of v0, /device:TPU:1, one launch (start us, length us, event | category | flops | bytes accessed | tf_op | source)
XLA Modules:
  0.0 849.2 jit_solution(7774384556777394916)
XLA Ops:
  8.2 6.8 fusion.70
  15.0 3.6 fusion.46
  21.1 3.6 copy.236
  27.2 9.9 %fusion.108 = f32[1024,1,4,2,32]{4,3,2,1,0:T(2,128)} fusion(f32[1,32,4,1,1024]{1,3,2,0,4:T(1,128)} %bitcast.341, f32[1,32,4,1,1024]{1,3,2,0,4:T(1,128)} %bitcast.339), kind=kLoop, calls=%fused_computation.186 | loop fusion | flops 262144 | bytes 2097152
  37.1 6.7 reshape.415
  43.8 11.3 %all-to-all-start = ((f32[32,1,8192]{2,1,0:T(1,128)}), f32[32,1,8192]{2,1,0:T(1,128)S(1)}, u32[]{:S(2)}, u32[]{:S(2)}) async-start(f32[32,1,8192]{2,1,0:T(1,128)} %reshape.415), calls=%async_computation | async-start | bytes 2097152 | tf_op jit(solution)/shard_map/all_to_all | solution.py:136
  55.2 17.2 %all-to-all-done = f32[32,1,8192]{2,1,0:T(1,128)S(1)} async-done(((f32[32,1,8192]{2,1,0:T(1,128)}), f32[32,1,8192]{2,1,0:T(1,128)S(1)}, u32[]{:S(2)}, u32[]{:S(2)}) %all-to-all-start) | async-done | bytes 1048608 | tf_op jit(solution)/shard_map/all_to_all | solution.py:136
  72.9 3.3 reduce.16
  76.2 4.9 reshape.416
  81.0 7.4 copy.238
  88.4 6.6 copy.146
  95.1 3.8 copy.147
  100.5 214.9 %all-gather.2.cloned.1.call-done = f32[2,32,32,32,32]{4,3,2,1,0:T(8,128)} async-done(((f32[2,32,32,8,32]{4,3,2,1,0:T(8,128)}), f32[2,32,32,32,32]{4,3,2,1,0:T(8,128)}) %all-gather.2.cloned.1.call-update) | async-done | bytes 8388624 | tf_op jit(solution)/shard_map/all_gather | solution.py:140
  315.5 13.5 %fusion.4 = (f32[32,32,32]{1,0,2:T(8,128)S(1)}, f32[32,32,32]{1,0,2:T(8,128)S(1)}, f32[32,32,32]{1,0,2:T(8,128)S(1)}, f32[32,32,32]{1,0,2:T(8,128)S(1)}) fusion(f32[2,32,32,32,32]{4,3,2,1,0:T(8,128)} %all-gather.2.cloned.1.call-done, f32[32,32,32]{1,0,2:T(8,128)S(1)} %copy.250, f32[32,32,32]{1,0,2:T(8,128)S(1)} %copy.249), kind=kLoop, calls=%fused_computation.11 | loop fusion | flops 8257536 | bytes 9175040
  333.5 4.3 copy.149
  337.8 6.5 reshape.417
  344.3 9.1 %all-to-all-start.1 = ((f32[32,1,8192]{2,1,0:T(1,128)}), f32[32,1,8192]{2,1,0:T(1,128)S(1)}, u32[]{:S(2)}, u32[]{:S(2)}) async-start(f32[32,1,8192]{2,1,0:T(1,128)} %reshape.417), calls=%async_computation.1 | async-start | bytes 2097152 | tf_op jit(solution)/shard_map/all_to_all | solution.py:144
  353.5 16.3 %fusion.21 = f32[32,4,128,128]{3,0,2,1:T(8,128)} fusion(f32[32,4,128,128]{3,2,1,0:T(8,128)} %bitcast.318, f32[32,32]{1,0:T(8,128)S(1)} %copy-done), kind=kOutput, calls=%fused_computation.37 | convolution fusion | flops 805306368 | bytes 16781312 | tf_op jit(solution)/shard_map/scpyz,co->sopyz/dot_general | solution.py:148
  371.3 3.3 reduce.17
  374.6 4.9 reshape.418
  379.5 7.9 copy.151
  393.1 3.4 fusion.53
  397.7 44.8 %fusion.13 = f32[32,4,128,128]{3,2,1,0:T(8,128)S(1)} fusion(bf16[1,32,4,128,128]{4,3,2,1,0:T(8,128)(2,1)S(1)} %copy-done.2, f32[32,4,128,128]{3,0,2,1:T(8,128)S(1)} %bitcast.338, f32[32]{0:T(128)S(1)} %copy-done.3, f32[1,32,4,128,32]{3,4,2,1,0:T(8,128)S(1)} %get-tuple-element.23, f32[1,32,4,128,32]{3,4,2,1,0:T(8,128)S(1)} %get-tuple-element.22, ...), kind=kOutput, calls=%fused_computation.27 | convolution fusion | flops 1766858752 | bytes 25198720 | tf_op jit(solution)/shard_map/scpyj,zj->scpyz/dot_general | solution.py:75
  442.6 3.4 copy-done.1
  446.0 5.3 fusion.67
  451.3 3.6 fusion.49
  457.4 3.4 copy.242
  463.3 8.9 %fusion.107 = f32[1024,1,4,2,32]{4,3,2,1,0:T(2,128)} fusion(f32[1,32,4,1,1024]{1,3,2,0,4:T(1,128)} %bitcast.342, f32[1,32,4,1,1024]{1,3,2,0,4:T(1,128)} %bitcast.340), kind=kLoop, calls=%fused_computation.185 | loop fusion | flops 262144 | bytes 2097152
  472.2 5.8 reshape.419
  478.0 26.0 %all_to_all.60 = f32[32,1,8192]{2,1,0:T(1,128)S(1)} all-to-all(f32[32,1,8192]{2,1,0:T(1,128)S(1)} %reshape.419), channel_id=1, replica_groups=mesh['dp'=4,'mp'=32] {'mp'}, dimensions={0} | all-to-all | bytes 2097152 | tf_op jit(solution)/shard_map/all_to_all | solution.py:153
  503.9 3.3 reduce.18
  507.2 4.9 reshape.420
  512.1 7.5 copy.244
  519.6 6.6 copy.160
  526.2 3.8 copy.161
  532.1 5.8 add_bitcast_fusion
  537.9 14.0 %pad_maximum_fusion = f32[2,32,32,32,32]{4,3,2,1,0:T(8,128)} fusion(f32[1,32,32,32,32]{4,3,2,1,0:T(8,128)S(1)} %get-tuple-element.29, f32[1,32,32,32,32]{4,3,2,1,0:T(8,128)S(1)} %get-tuple-element.28), kind=kLoop, calls=%fused_computation | loop fusion | flops 2097152 | bytes 16777216 | tf_op jit(solution)/shard_map/stack | solution.py:117
  552.0 15.6 %fusion.1 = (f32[32,32,32]{1,0,2:T(8,128)S(1)}, f32[32,32,32]{1,0,2:T(8,128)S(1)}, f32[32,32,32]{1,0,2:T(8,128)S(1)}, f32[32,32,32]{1,0,2:T(8,128)S(1)}) fusion(f32[2,32,32,32,32]{4,3,2,1,0:T(8,128)} %all-gather.2.cloned.1.call-done, f32[32,32,32]{1,0,2:T(8,128)S(1)} %copy.251, f32[32,32,32]{1,0,2:T(8,128)S(1)} %copy.252), kind=kLoop, calls=%fused_computation.4 | loop fusion | flops 8257536 | bytes 9175040
  571.7 4.5 copy.164
  576.3 6.5 reshape.421
  582.8 5.6 all-to-all-start.3
  588.4 17.7 %fusion.18 = f32[4,128,128,32]{2,3,1,0:T(8,128)} fusion(f32[32,4,128,128]{3,2,1,0:T(8,128)} %copy-done.1, f32[32,32]{1,0:T(8,128)S(1)} %copy-done), kind=kOutput, calls=%fused_computation.33 | convolution fusion | flops 805306368 | bytes 16781312 | tf_op jit(solution)/shard_map/sopyz,co->scpyz/dot_general | solution.py:167
  606.1 3.3 reduce.19
  609.4 4.9 reshape.422
  614.3 7.8 copy.166
  627.8 3.4 fusion.52
  631.8 22.5 %fusion.17 = f32[1,32,4,128,128]{4,3,2,1,0:T(8,128)} fusion(f32[4,128,128,32]{2,3,1,0:T(8,128)S(1)} %bitcast.320, f32[1,32,4,128,32]{3,4,2,1,0:T(8,128)S(1)} %get-tuple-element.17, f32[1,32,4,128,32]{3,4,2,1,0:T(8,128)S(1)} %get-tuple-element.16, f32[128,32]{0,1:T(8,128)S(1)} %get-tuple-element.48, f32[128,32]{0,1:T(8,128)S(1)} %get-tuple-element.49), kind=kOutput, calls=%fused_computation.32 | convolution fusion | flops 1613766656 | bytes 21004288 | tf_op jit(solution)/shard_map/scpyj,zj->scpyz/dot_general | solution.py:75
  654.3 187.8 %reduce-scatter.2.cloned.1.call-done = f32[2,32,32,8,32]{4,3,2,1,0:T(8,128)} async-done(((f32[2,32,32,32,32]{4,3,2,1,0:T(8,128)}), f32[2,32,32,8,32]{4,3,2,1,0:T(8,128)}) %reduce-scatter.2.cloned.1.call-update) | async-done | bytes 2097168 | tf_op jit(solution)/shard_map/reduce_scatter | solution.py:159
  (70 shorter events, 38.4 us)
Async XLA Ops:
  7.2 346.3 %copy-start = (f32[32,32]{1,0:T(8,128)S(1)}, f32[32,32]{1,0:T(8,128)}, u32[]{:S(2)}) copy-start(f32[32,32]{1,0:T(8,128)} %param.8) | copy-start | bytes 12292
  7.2 308.3 %all-gather.2.cloned.1.call-start = ((), (), s32[]{:S(2)}) async-start(), calls=%async_computation.5 | async-start | bytes 41943040 | tf_op jit(solution)/shard_map/all_gather | solution.py:140
  43.8 28.5 %all-to-all-start = ((f32[32,1,8192]{2,1,0:T(1,128)}), f32[32,1,8192]{2,1,0:T(1,128)S(1)}, u32[]{:S(2)}, u32[]{:S(2)}) async-start(f32[32,1,8192]{2,1,0:T(1,128)} %reshape.415), calls=%async_computation | async-start | bytes 2097152 | tf_op jit(solution)/shard_map/all_to_all | solution.py:136
  344.3 27.0 %all-to-all-start.1 = ((f32[32,1,8192]{2,1,0:T(1,128)}), f32[32,1,8192]{2,1,0:T(1,128)S(1)}, u32[]{:S(2)}, u32[]{:S(2)}) async-start(f32[32,1,8192]{2,1,0:T(1,128)} %reshape.417), calls=%async_computation.1 | async-start | bytes 2097152 | tf_op jit(solution)/shard_map/all_to_all | solution.py:144
  353.4 488.6 %reduce-scatter.2.cloned.1.call-start = ((), (), s32[]{:S(2)}) async-start(), calls=%async_computation.6 | async-start | bytes 41943040 | tf_op jit(solution)/shard_map/reduce_scatter | solution.py:159
  393.1 4.2 slice-start.2
  393.1 4.2 slice-start.3
  393.1 4.6 copy-start.2
  393.1 4.6 copy-start.3
  442.6 3.4 copy-start.1
  582.8 23.4 %all-to-all-start.3 = ((f32[32,1,8192]{2,1,0:T(1,128)}), f32[32,1,8192]{2,1,0:T(1,128)S(1)}, u32[]{:S(2)}, u32[]{:S(2)}) async-start(f32[32,1,8192]{2,1,0:T(1,128)} %reshape.421), calls=%async_computation.3 | async-start | bytes 2097152 | tf_op jit(solution)/shard_map/all_to_all | solution.py:163
  627.8 3.9 slice-start
  627.8 3.9 slice-start.1
Sparse Core Ops, SparseCore 0:
  9.7 305.7 all-gather.1
  552.1 289.8 reduce-scatter.1
where the time goes:
time: 857 us; the launch traced here: 849 us
  waiting for transfers between devices  422 us (49%)
  local copies, waits for them, and re-layouts  131 us (15%)
  matrix products  131 us (15%)
  other arithmetic  97.4 us (11%)
  starting transfers between devices  26.2 us (3%)
  blocking collectives  26 us (3%)
  between operations  15 us (2%)
    all_gather x1, waiting for transfers between devices, shards(): full_weight = lax.all_gather(spectral_weight, 'dp', axis=3, tiled=True)  215 us
    reduce_scatter x1, waiting for transfers between devices, shards(): lax.psum_scatter(weight_gradient(grad_spec, spectrum), 'dp', scatter_dime...  188 us
    dot_general x2, matrix products, inverse_plane(): return jnp.einsum('scpyj,zj->scpyz', merged, table_z, precision=HIGHEST)  67.3 us
    unnamed x29, local copies, waits for them, and re-layouts  49.8 us
    unnamed x7, other arithmetic  48.2 us
    all_to_all x1, blocking collectives, shards(): lax.all_to_all(forward_plane(grad_pre, table_y, table_z), 'mp', split_axi...  26 us
    another operation x2, other arithmetic, weight_gradient(): return jnp.stack([real_part, imag_part], axis=0)  19.8 us
    dot_general x1, matrix products, shards(): jnp.einsum('sopyz,co->scpyz', grad_pre, point_weight, precision=HIGHEST)  17.7 us
  transfers between devices with their start and end apart: 5, of which 4 were waited for; matrix products, arithmetic and copies ran while one was open for 21% of the time, Pallas kernels for 0%

commit v1 on v0

v1 whole, which is shorter than its diff:
```python
from functools import partial

import jax
import jax.numpy as jnp
import ml_dtypes
import numpy as np
from jax import lax
from jax.experimental import pallas as pl
from jax.experimental.pallas import tpu as pltpu
from jax.sharding import PartitionSpec as P

N = 128
M = 32
C = 32
XL = 4
CG = 8
DP = 4
MP = 32
F32 = jnp.float32
BF16 = jnp.bfloat16
VMEM_LIMIT = 60 * 1024 * 1024


def split_np(table):
    table = table.astype(np.float32)
    high = table.astype(ml_dtypes.bfloat16)
    low = (table - high.astype(np.float32)).astype(ml_dtypes.bfloat16)
    return high, low


def angles(signed):
    frequency = np.arange(M)
    if signed:
        frequency = np.where(frequency < M // 2, frequency, frequency - M)
    phase = (np.arange(N)[:, None] * frequency[None, :]) % N
    theta = phase * (2.0 * np.pi / N)
    return np.cos(theta), np.sin(theta)


def make_tables():
    cz, sz = angles(False)
    cs, ss = angles(True)
    tz = np.zeros((4, N, 2, 4, M))
    for c in range(4):
        tz[c, :, 0, c, :] = cz
        tz[c, :, 1, c, :] = sz
    tz = tz.reshape(4 * N, 8 * M)
    ty = np.block([[cs.T, -ss.T], [-ss.T, -cs.T]])
    tx = np.zeros((2, M, N, 2))
    tx[0, :, :, 0] = cs.T
    tx[0, :, :, 1] = ss.T
    tx[1, :, :, 0] = -ss.T
    tx[1, :, :, 1] = cs.T
    tx = tx.reshape(2 * M, 2 * N)
    ix = np.zeros((N, 2, 2, M))
    ix[:, 0, 0] = cs
    ix[:, 0, 1] = -ss
    ix[:, 1, 0] = ss
    ix[:, 1, 1] = cs
    ix = ix.reshape(2 * N, 2 * M)
    iy = np.block([[cs, -ss], [ss, cs]])
    iz = np.zeros((2, 4, M, 4, N))
    for c in range(4):
        iz[0, c, :, c, :] = cz.T
        iz[1, c, :, c, :] = -sz.T
    iz = iz.reshape(8 * M, 4 * N)
    expand = np.repeat(np.eye(C), 8, axis=0)
    return {
        "tz": split_np(tz),
        "ty": split_np(ty),
        "tx": split_np(tx),
        "ix": split_np(ix),
        "iy": split_np(iy),
        "iz": split_np(iz),
        "expand": expand.astype(np.float32),
    }


TABLES = make_tables()


def split(value):
    high = value.astype(BF16)
    low = (value - high.astype(F32)).astype(BF16)
    return high, low


def mm(a, b):
    return jnp.dot(a, b, preferred_element_type=F32)


def left_table(table_h, table_l, data):
    high, low = split(data)
    return mm(table_h, high) + (mm(table_h, low) + mm(table_l, high))


def right_table(data, table_h, table_l):
    high, low = split(data)
    return mm(high, table_h) + (mm(low, table_h) + mm(high, table_l))


def params(limit=VMEM_LIMIT):
    return pltpu.CompilerParams(vmem_limit_bytes=limit)


def whole(shape):
    return pl.BlockSpec(shape, lambda *_: (0,) * len(shape))


def forward_tile(channels, tz_h, tz_l, ty_h, ty_l):
    rows = jnp.concatenate(channels, axis=1)
    along_z = right_table(rows, tz_h, tz_l)
    stacked = jnp.concatenate([along_z[:, :N], along_z[:, N:]], axis=0)
    return left_table(ty_h, ty_l, stacked)


def inverse_tile(modes, iy_h, iy_l, iz_h, iz_l):
    along_y = left_table(iy_h, iy_l, modes)
    merged = jnp.concatenate([along_y[:N], along_y[N:]], axis=1)
    return right_table(merged, iz_h, iz_l)


def factor_lanes():
    lane = lax.broadcasted_iota(jnp.int32, (8, N), 1)
    return jnp.where(lane % M == 0, 1.0, 2.0).astype(F32) * (1.0 / float(N * N * N))


def forward_plane_kernel(field_ref, tz_h, tz_l, ty_h, ty_l, out_ref):
    group = pl.program_id(0)
    tzh, tzl, tyh, tyl = tz_h[...], tz_l[...], ty_h[...], ty_l[...]
    for x in range(XL):
        tile = forward_tile([field_ref[c, x] for c in range(4)], tzh, tzl, tyh, tyl)
        for r in range(2):
            out_ref[pl.ds(group * 8 + 2 * x + r, M, stride=8 * CG), :] = tile[
                r * M : (r + 1) * M
            ]


def forward_plane(fields):
    tz, ty = TABLES["tz"], TABLES["ty"]
    return pl.pallas_call(
        forward_plane_kernel,
        grid=(CG,),
        in_specs=[
            pl.BlockSpec((4, XL, N, N), lambda g: (g, 0, 0, 0)),
            whole((4 * N, 8 * M)),
            whole((4 * N, 8 * M)),
            whole((2 * M, 2 * N)),
            whole((2 * M, 2 * N)),
        ],
        out_specs=whole((M * CG * 8, N)),
        out_shape=jax.ShapeDtypeStruct((M * CG * 8, N), F32),
        compiler_params=params(),
    )(fields, *map(jnp.asarray, tz + ty)).reshape(M, CG, 8, N)


def forward_x_kernel(in_ref, tx_h, tx_l, out_ref):
    txh, txl = tx_h[...], tx_l[...]
    for g in range(CG):
        tile = left_table(txh, txl, in_ref[:, g].reshape(2 * N, N))
        for r in range(2):
            for d in range(DP):
                out_ref[d, g, r] = tile[r * M + 8 * d : r * M + 8 * d + 8]


def forward_x(pieces):
    return pl.pallas_call(
        forward_x_kernel,
        out_shape=jax.ShapeDtypeStruct((DP, CG, 2, 8, N), F32),
        compiler_params=params(),
    )(pieces, *map(jnp.asarray, TABLES["tx"]))


def inverse_x_kernel(in_ref, ix_h, ix_l, out_ref):
    ixh, ixl = ix_h[...], ix_l[...]
    for g in range(CG):
        rows = jnp.concatenate(
            [in_ref[:, g, 0].reshape(M, N), in_ref[:, g, 1].reshape(M, N)], axis=0
        )
        out_ref[:, g] = left_table(ixh, ixl, rows).reshape(MP, 8, N)


def inverse_x(pieces):
    return pl.pallas_call(
        inverse_x_kernel,
        out_shape=jax.ShapeDtypeStruct((MP, CG, 8, N), F32),
        compiler_params=params(),
    )(pieces, *map(jnp.asarray, TABLES["ix"]))


def pack_kernel(w_ref, out_ref):
    @pl.loop(0, C)
    def _(o):
        for r in range(2):
            for g in range(w_ref.shape[1] // 4):
                out_ref[r, g, o] = jnp.concatenate(
                    [w_ref[r, 4 * g + q, o] for q in range(4)], axis=1
                )


def pack_weight(weight):
    return pl.pallas_call(
        pack_kernel,
        grid=(4,),
        in_specs=[pl.BlockSpec((2, 8, C, 8, M), lambda i: (0, i, 0, 0, 0))],
        out_specs=pl.BlockSpec((2, 2, C, 8, N), lambda i: (0, i, 0, 0, 0)),
        out_shape=jax.ShapeDtypeStruct((2, CG, C, 8, N), F32),
        compiler_params=params(),
    )(weight)


def lane_groups():
    return lax.broadcasted_iota(jnp.int32, (8, N), 1) // M


def pick(groups, tiles):
    low = jnp.where(groups == 0, tiles[0], tiles[1])
    high = jnp.where(groups == 2, tiles[2], tiles[3])
    return jnp.where(groups < 2, low, high)


def mix_kernel(spec_ref, w_ref, out_ref):
    groups = lane_groups()
    factor = factor_lanes()

    @pl.loop(0, CG)
    def _(g):
        totals = [[[] for _ in range(2)] for _ in range(DP)]
        for q in range(4):
            o = 4 * g + q
            acc = [[None, None] for _ in range(DP)]
            for i in range(CG):
                wr, wi = w_ref[0, i, o], w_ref[1, i, o]
                for b in range(DP):
                    sr, si = spec_ref[b, i, 0], spec_ref[b, i, 1]
                    re = wr * sr - wi * si
                    im = wr * si + wi * sr
                    acc[b] = [re, im] if i == 0 else [acc[b][0] + re, acc[b][1] + im]
            for b in range(DP):
                for r in range(2):
                    v = acc[b][r]
                    v = v + pltpu.roll(v, 64, 1)
                    totals[b][r].append(v + pltpu.roll(v, 32, 1))
        for b in range(DP):
            for r in range(2):
                out_ref[b, g, r] = pick(groups, totals[b][r]) * factor


def mix(spectrum, weight):
    return pl.pallas_call(
        mix_kernel,
        out_shape=jax.ShapeDtypeStruct((DP, CG, 2, 8, N), F32),
        compiler_params=params(),
    )(spectrum, weight)


def spread(grad_ref, rep_ref):
    groups = lane_groups()
    factor = factor_lanes()

    @pl.loop(0, CG)
    def _(g):
        for b in range(DP):
            for r in range(2):
                v = grad_ref[b, g, r] * factor
                rolled = [v] + [pltpu.roll(v, M * s, 1) for s in range(1, 4)]
                for q in range(4):
                    rep_ref[4 * g + q, b, r] = pick(
                        groups, [rolled[(h - q) % 4] for h in range(4)]
                    )


def back_mix_kernel(grad_ref, w_ref, out_ref, rep_ref):
    spread(grad_ref, rep_ref)

    @pl.loop(0, CG)
    def _(i):
        def step(t, acc):
            acc = list(acc)
            for u in range(4):
                o = 4 * t + u
                wr, wi = w_ref[0, i, o], w_ref[1, i, o]
                for b in range(DP):
                    gr, gi = rep_ref[o, b, 0], rep_ref[o, b, 1]
                    acc[2 * b] = acc[2 * b] + (wr * gr + wi * gi)
                    acc[2 * b + 1] = acc[2 * b + 1] + (wr * gi - wi * gr)
            return tuple(acc)

        acc = lax.fori_loop(0, 8, step, tuple(jnp.zeros((8, N), F32) for _ in range(8)))
        for b in range(DP):
            for r in range(2):
                out_ref[b, i, r] = acc[2 * b + r]


def back_mix(grad_spec, weight):
    return pl.pallas_call(
        back_mix_kernel,
        out_shape=jax.ShapeDtypeStruct((DP, CG, 2, 8, N), F32),
        scratch_shapes=[pltpu.VMEM((C, DP, 2, 8, N), F32)],
        compiler_params=params(),
    )(grad_spec, weight)


def weight_grad_kernel(grad_ref, spec_ref, out_ref, rep_ref):
    @pl.when(pl.program_id(0) == 0)
    def _():
        spread(grad_ref, rep_ref)

    @pl.loop(0, C)
    def _(o):
        for g in range(2):
            re = im = None
            for b in range(DP):
                gr, gi = rep_ref[o, b, 0], rep_ref[o, b, 1]
                sr, si = spec_ref[b, g, 0], spec_ref[b, g, 1]
                r1 = gr * sr + gi * si
                i1 = gi * sr - gr * si
                re, im = (r1, i1) if b == 0 else (re + r1, im + i1)
            for q in range(4):
                out_ref[0, 4 * g + q, o] = re[:, M * q : M * (q + 1)]
                out_ref[1, 4 * g + q, o] = im[:, M * q : M * (q + 1)]


def weight_grad(grad_spec, spectrum):
    return pl.pallas_call(
        weight_grad_kernel,
        grid=(4,),
        in_specs=[
            whole((DP, CG, 2, 8, N)),
            pl.BlockSpec((DP, 2, 2, 8, N), lambda i: (0, i, 0, 0, 0)),
        ],
        out_specs=pl.BlockSpec((2, 8, C, 8, M), lambda i: (0, i, 0, 0, 0)),
        out_shape=jax.ShapeDtypeStruct((2, C, C, 8, M), F32),
        scratch_shapes=[pltpu.VMEM((C, DP, 2, 8, N), F32)],
        compiler_params=params(),
    )(grad_spec, spectrum)


def channel_matrix(matrix, expand):
    spread_cols = lax.dot_general(
        matrix, expand, (((1,), (1,)), ((), ())), precision=lax.Precision.HIGHEST
    )
    full = jnp.dot(expand, spread_cols, precision=lax.Precision.HIGHEST)
    row = lax.broadcasted_iota(jnp.int32, (8 * C, 8 * C), 0)
    col = lax.broadcasted_iota(jnp.int32, (8 * C, 8 * C), 1)
    return split(jnp.where(row % 8 == col % 8, full, 0.0))


def spectral_plane(modes_ref, x, out_ref, tables):
    @pl.loop(0, CG)
    def _(g):
        modes = jnp.concatenate(
            [
                modes_ref[pl.ds(g * 8 + 2 * x + r, M, stride=8 * CG), :]
                for r in range(2)
            ],
            axis=0,
        )
        plane = inverse_tile(modes, *[t[...] for t in tables])
        for q in range(4):
            out_ref[4 * g + q] = plane[:, q * N : (q + 1) * N]


def channel_map(in_ref, y, mat_h, mat_l):
    data = jnp.concatenate(
        [in_ref[:, pl.ds(y + 8 * h, 8), :].reshape(8 * C, N) for h in range(2)], axis=1
    )
    return left_table(mat_h, mat_l, data)


def forward_cell_kernel(
    modes_ref, field_ref, up_ref, pw_ref, bias_ref, ex_ref,
    iy_h, iy_l, iz_h, iz_l, tz_h, tz_l, ty_h, ty_l,
    grad_ref, out_ref, mat_h, mat_l, pre_ref,
):
    x = pl.program_id(0)

    @pl.when(x == 0)
    def _():
        mat_h[...], mat_l[...] = channel_matrix(pw_ref[...].T, ex_ref[...])

    spectral_plane(modes_ref, x, pre_ref, (iy_h, iy_l, iz_h, iz_l))

    @pl.loop(0, N // 16)
    def _(t):
        y = pl.multiple_of(t * 16, 16)
        mapped = channel_map(field_ref, y, mat_h[...], mat_l[...])
        point = jnp.concatenate(
            [mapped[:, :N].reshape(C, 8, N), mapped[:, N:].reshape(C, 8, N)], axis=1
        )
        pre = pre_ref[:, pl.ds(y, 16), :] + point + bias_ref[...]
        cdf = 0.5 * (1.0 + lax.erf(pre * np.float32(np.sqrt(0.5))))
        slope = cdf + pre * (jnp.exp(-0.5 * pre * pre) * np.float32(1 / np.sqrt(2 * np.pi)))
        grad_ref[:, pl.ds(y, 16), :] = up_ref[:, pl.ds(y, 16), :].astype(F32) * slope

    @pl.loop(0, CG)
    def _(g):
        tile = forward_tile(
            [grad_ref[4 * g + q] for q in range(4)], tz_h[...], tz_l[...], ty_h[...], ty_l[...]
        )
        for r in range(2):
            out_ref[pl.ds(g * 8 + 2 * x + r, M, stride=8 * CG), :] = tile[r * M : (r + 1) * M]


def plane_spec():
    return pl.BlockSpec((C, pl.Squeezed(), N, N), lambda x: (0, x, 0, 0))


def forward_cells(modes, fields, upstream, point_weight, point_bias):
    tabs = TABLES["iy"] + TABLES["iz"] + TABLES["tz"] + TABLES["ty"]
    grad_pre, out = pl.pallas_call(
        forward_cell_kernel,
        grid=(XL,),
        in_specs=[
            whole((M * CG * 8, N)),
            plane_spec(),
            plane_spec(),
            whole((C, C)),
            whole((C, 1, N)),
            whole((8 * C, C)),
        ]
        + [whole(t.shape) for t in tabs],
        out_specs=[plane_spec(), whole((M * CG * 8, N))],
        out_shape=[
            jax.ShapeDtypeStruct((C, XL, N, N), F32),
            jax.ShapeDtypeStruct((M * CG * 8, N), F32),
        ],
        scratch_shapes=[
            pltpu.VMEM((8 * C, 8 * C), BF16),
            pltpu.VMEM((8 * C, 8 * C), BF16),
            pltpu.VMEM((C, N, N), F32),
        ],
        compiler_params=params(),
    )(
        modes.reshape(M * CG * 8, N),
        fields,
        upstream,
        point_weight,
        jnp.broadcast_to(point_bias[:, None, None], (C, 1, N)),
        jnp.asarray(TABLES["expand"]),
        *map(jnp.asarray, tabs),
    )
    return grad_pre, out.reshape(M, CG, 8, N)


def backward_cell_kernel(
    modes_ref, grad_ref, pw_ref, ex_ref, iy_h, iy_l, iz_h, iz_l, out_ref, mat_h, mat_l
):
    x = pl.program_id(0)

    @pl.when(x == 0)
    def _():
        mat_h[...], mat_l[...] = channel_matrix(pw_ref[...], ex_ref[...])

    spectral_plane(modes_ref, x, out_ref, (iy_h, iy_l, iz_h, iz_l))

    @pl.loop(0, N // 16)
    def _(t):
        y = pl.multiple_of(t * 16, 16)
        mapped = channel_map(grad_ref, y, mat_h[...], mat_l[...])
        for h in range(2):
            at = pl.ds(y + 8 * h, 8)
            out_ref[:, at, :] = out_ref[:, at, :] + mapped[:, h * N : (h + 1) * N].reshape(C, 8, N)


def backward_cells(modes, grad_pre, point_weight):
    tabs = TABLES["iy"] + TABLES["iz"]
    return pl.pallas_call(
        backward_cell_kernel,
        grid=(XL,),
        in_specs=[whole((M * CG * 8, N)), plane_spec(), whole((C, C)), whole((8 * C, C))]
        + [whole(t.shape) for t in tabs],
        out_specs=plane_spec(),
        out_shape=jax.ShapeDtypeStruct((C, XL, N, N), F32),
        scratch_shapes=[pltpu.VMEM((8 * C, 8 * C), BF16), pltpu.VMEM((8 * C, 8 * C), BF16)],
        compiler_params=params(),
    )(
        modes.reshape(M * CG * 8, N),
        grad_pre,
        point_weight,
        jnp.asarray(TABLES["expand"]),
        *map(jnp.asarray, tabs),
    )


def swap(pieces, axis):
    return lax.all_to_all(pieces, axis, split_axis=0, concat_axis=0, tiled=True)


def shards(fields, upstream, spectral_weight, point_weight, point_bias):
    fields = fields[0]
    upstream = upstream[0]
    weight = pack_weight(spectral_weight)
    spectrum = swap(forward_x(swap(forward_plane(fields), "mp")), "dp")
    mixed = mix(spectrum, weight)
    modes = swap(inverse_x(swap(mixed, "dp")), "mp")
    grad_pre, pieces = forward_cells(modes, fields, upstream, point_weight, point_bias)
    grad_spec = swap(forward_x(swap(pieces, "mp")), "dp")
    back = back_mix(grad_spec, weight)
    weight_out = weight_grad(grad_spec, spectrum)
    modes = swap(inverse_x(swap(back, "dp")), "mp")
    grad_fields = backward_cells(modes, grad_pre, point_weight)
    return (grad_fields[None], weight_out)


def solution(mesh):
    placed = (
        P("dp", None, "mp", None, None),
        P("dp", None, "mp", None, None),
        P(None, None, None, "dp", "mp"),
        P(),
        P(),
    )
    return jax.shard_map(
        shards,
        mesh=mesh,
        in_specs=placed,
        out_specs=(P("dp", None, "mp", None, None), P(None, None, None, "dp", "mp")),
        check_vma=False,
    )
```

time: 857 us -> 258 us (0.30)
  waiting for transfers between devices: 422 us -> 2.27 us
  Pallas kernels: 0 us -> 139 us
  matrix products: 131 us -> 0 us
  local copies, waits for them, and re-layouts: 131 us -> 2.43 us
  other arithmetic: 97.4 us -> 0 us
  blocking collectives: 26 us -> 102 us
  starting transfers between devices: 26.2 us -> 9.83 us
  between operations: 15 us -> 0.65 us
    all_gather x1 -> x0, waiting for transfers between devices: 215 us -> none  [shards(): full_weight = lax.all_gather(spectral_weight, 'dp', axis=3, tiled=True)]
    reduce_scatter x1 -> x0, waiting for transfers between devices: 188 us -> none  [shards(): lax.psum_scatter(weight_gradient(grad_spec, spectrum), 'dp', scatter_dime...]
    pallas_call x0 -> x11, Pallas kernels: none -> 139 us  [the longest x1 48.7 us: forward_cells(): pl.pallas_call(forward_cell_kernel, grid=(XL,), in_specs=[whole((M * CG *...]
    dot_general x12 -> x0, matrix products: 129 us -> none  [the longest x2 67.3 us: inverse_plane(): return jnp.einsum('scpyj,zj->scpyz', merged, table_z, precision=HIGHEST)]
    all_to_all x1 -> x6, blocking collectives: 26 us -> 102 us  [swap(): return lax.all_to_all(pieces, axis, split_axis=0, concat_axis=0, tiled=True)]
    unnamed x7 -> x0, other arithmetic: 48.2 us -> none
    unnamed x29 -> x6, local copies, waits for them, and re-layouts: 49.8 us -> 1.73 us
    all_to_all x7 -> x0, local copies, waits for them, and re-layouts: 44.5 us -> none  [the longest x3 14.6 us: shards(): lax.all_to_all(forward_plane(fields, table_y, table_z), 'mp', split_axis=...]
  transfers between devices with their start and end apart: 5 -> 2, of which waited for: 4 -> 1; matrix products, arithmetic and copies ran while one was open for 21% -> 0% of each run, Pallas kernels for 0% -> 11%
where the time goes in v1:
time: 258 us; the launch traced here: 256 us
  Pallas kernels  139 us (54%)
  blocking collectives  102 us (40%)
  starting transfers between devices  9.83 us (4%)
    all_to_all x6, blocking collectives, swap(): return lax.all_to_all(pieces, axis, split_axis=0, concat_axis=0, tiled=True)  102 us
    pallas_call x1, Pallas kernels, forward_cells(): pl.pallas_call(forward_cell_kernel, grid=(XL,), in_specs=[whole((M * CG *...  48.7 us
    pallas_call x1, Pallas kernels, backward_cells(): pl.pallas_call(backward_cell_kernel, grid=(XL,), in_specs=[whole((M * CG...  29.3 us
    pallas_call x1, Pallas kernels, forward_plane(): pl.pallas_call(forward_plane_kernel, grid=(CG,), in_specs=[pl.BlockSpec((...  15.1 us
    pallas_call x1, Pallas kernels, weight_grad(): pl.pallas_call(weight_grad_kernel, grid=(4,), in_specs=[whole((DP, CG, 2,...  14.3 us
    pallas_call x1, Pallas kernels, pack_weight(): pl.pallas_call(pack_kernel, grid=(4,), in_specs=[pl.BlockSpec((2, 8, C, 8...  12.8 us
    all_to_all x2, starting transfers between devices, swap(): return lax.all_to_all(pieces, axis, split_axis=0, concat_axis=0, tiled=True)  9.83 us
  transfers between devices with their start and end apart: 2, of which 1 were waited for; matrix products, arithmetic and copies ran while one was open for 0% of the time, Pallas kernels for 11%

profile of v1, /device:TPU:1, one launch (start us, length us, event | category | flops | bytes accessed | tf_op | source)
XLA Modules:
  0.0 256.1 jit_solution(9840435366774468111)
XLA Ops:
  0.6 15.1 %shard_map.185 = f32[2048,128]{1,0:T(8,128)} custom-call(f32[32,4,128,128]{3,2,1,0:T(8,128)} %bitcast.7, bf16[512,256]{1,0:T(8,128)(2,1)} %constant.26.clone.tz_h, bf16[512,256]{1,0:T(8,128)(2,1)} %constant.27.clone.tz_l, bf16[64,256]{1,0:T(8,128)(2,1)} %constant.28.clone.ty_h, bf16[64,256]{1,0:T(8,128)(2,1)} %constant.29.clone.ty_l), custom_call_target="tpu_custom_call" | custom-call | tf_op jit(solution)/shard_map/pallas_call | solution.py:141
  15.7 28.2 %all_to_all.40.in_ref = f32[32,8,8,128]{3,2,1,0:T(8,128)} all-to-all(f32[32,8,8,128]{3,2,1,0:T(8,128)} %bitcast.12), channel_id=1, replica_groups=mesh['dp'=4,'mp'=32] {'mp'}, dimensions={0} | all-to-all | bytes 2097152 | tf_op jit(solution)/shard_map/all_to_all | solution.py:487
  43.9 2.3 shard_map.186
  46.2 5.5 %all-to-all-start.1 = ((f32[4,8,2,8,128]{4,3,2,1,0:T(8,128)}), f32[4,8,2,8,128]{4,3,2,1,0:T(8,128)S(1)}, u32[]{:S(2)}, u32[]{:S(2)}) async-start(f32[4,8,2,8,128]{4,3,2,1,0:T(8,128)} %shard_map.186), calls=%async_computation.1 | async-start | bytes 524288 | tf_op jit(solution)/shard_map/all_to_all | solution.py:487
  51.8 0.0 copy-start.2
  51.8 12.8 %shard_map.187.w_ref = f32[2,8,32,8,128]{4,3,2,1,0:T(8,128)} custom-call(f32[2,32,32,8,32]{4,3,2,1,0:T(8,128)} %w_ref.1), custom_call_target="tpu_custom_call" | custom-call | tf_op jit(solution)/shard_map/pallas_call | solution.py:202
  64.6 0.0 all-to-all-done.1.spec_ref
  64.6 0.0 copy-start.1
  64.6 0.7 copy-done.1
  65.2 4.7 %shard_map.188 = f32[4,8,2,8,128]{4,3,2,1,0:T(8,128)} custom-call(f32[4,8,2,8,128]{4,3,2,1,0:T(8,128)} %copy-done.1, f32[2,8,32,8,128]{4,3,2,1,0:T(8,128)} %shard_map.187.w_ref), custom_call_target="tpu_custom_call" | custom-call | tf_op jit(solution)/shard_map/pallas_call | solution.py:250
  69.9 9.1 %all_to_all.41.in_ref = f32[4,8,2,8,128]{4,3,2,1,0:T(8,128)} all-to-all(f32[4,8,2,8,128]{4,3,2,1,0:T(8,128)} %shard_map.188), channel_id=1, replica_groups=mesh['dp'=4,'mp'=32] {'dp'}, dimensions={0} | all-to-all | bytes 524288 | tf_op jit(solution)/shard_map/all_to_all | solution.py:487
  79.1 2.5 shard_map.189
  81.6 21.3 %all_to_all.42 = f32[32,8,8,128]{3,2,1,0:T(8,128)} all-to-all(f32[32,8,8,128]{3,2,1,0:T(8,128)} %shard_map.189), channel_id=1, replica_groups=mesh['dp'=4,'mp'=32] {'mp'}, dimensions={0} | all-to-all | bytes 2097152 | tf_op jit(solution)/shard_map/all_to_all | solution.py:487
  102.9 0.0 copy-done.2
  102.9 0.7 broadcast_in_dim.4.bias_ref
  103.6 48.7 %shard_map.190 = (f32[32,4,128,128]{3,2,1,0:T(8,128)}, f32[2048,128]{1,0:T(8,128)}) custom-call(f32[2048,128]{1,0:T(8,128)} %bitcast.10, f32[32,4,128,128]{3,2,1,0:T(8,128)} %bitcast.8, bf16[32,4,128,128]{3,2,1,0:T(8,128)(2,1)} %bitcast.11, f32[32,32]{1,0:T(8,128)} %pw_ref.3, f32[32,1,128]{2,1,0:T(1,128)} %broadcast_in_dim.4.bias_ref, ...), custom_call_target="tpu_custom_call" | custom-call | tf_op jit(solution)/shard_map/pallas_call | solution.py:411
  152.2 20.2 %all_to_all.43.in_ref = f32[32,8,8,128]{3,2,1,0:T(8,128)} all-to-all(f32[32,8,8,128]{3,2,1,0:T(8,128)} %bitcast.14), channel_id=1, replica_groups=mesh['dp'=4,'mp'=32] {'mp'}, dimensions={0} | all-to-all | bytes 2097152 | tf_op jit(solution)/shard_map/all_to_all | solution.py:487
  172.4 2.3 shard_map.191
  174.8 12.9 %all_to_all.44.grad_ref = f32[4,8,2,8,128]{4,3,2,1,0:T(8,128)} all-to-all(f32[4,8,2,8,128]{4,3,2,1,0:T(8,128)} %shard_map.191), channel_id=1, replica_groups=mesh['dp'=4,'mp'=32] {'dp'}, dimensions={0} | all-to-all | bytes 524288 | tf_op jit(solution)/shard_map/all_to_all | solution.py:487
  187.6 4.6 %shard_map.192 = f32[4,8,2,8,128]{4,3,2,1,0:T(8,128)} custom-call(f32[4,8,2,8,128]{4,3,2,1,0:T(8,128)} %all_to_all.44.grad_ref, f32[2,8,32,8,128]{4,3,2,1,0:T(8,128)} %shard_map.187.w_ref), custom_call_target="tpu_custom_call" | custom-call | tf_op jit(solution)/shard_map/pallas_call | solution.py:296
  192.3 10.1 %all_to_all.45.in_ref = f32[4,8,2,8,128]{4,3,2,1,0:T(8,128)} all-to-all(f32[4,8,2,8,128]{4,3,2,1,0:T(8,128)} %shard_map.192), channel_id=1, replica_groups=mesh['dp'=4,'mp'=32] {'dp'}, dimensions={0} | all-to-all | bytes 524288 | tf_op jit(solution)/shard_map/all_to_all | solution.py:487
  202.4 2.5 shard_map.193
  204.9 4.3 %all-to-all-start.7 = ((f32[32,8,8,128]{3,2,1,0:T(8,128)}), f32[32,8,8,128]{3,2,1,0:T(8,128)S(1)}, u32[]{:S(2)}, u32[]{:S(2)}) async-start(f32[32,8,8,128]{3,2,1,0:T(8,128)} %shard_map.193), calls=%async_computation.7 | async-start | bytes 2097152 | tf_op jit(solution)/shard_map/all_to_all | solution.py:487
  209.2 14.3 %shard_map.195 = f32[2,32,32,8,32]{4,3,2,1,0:T(8,128)} custom-call(f32[4,8,2,8,128]{4,3,2,1,0:T(8,128)} %all_to_all.44.grad_ref, f32[4,8,2,8,128]{4,3,2,1,0:T(8,128)} %copy-done.1), custom_call_target="tpu_custom_call" | custom-call | tf_op jit(solution)/shard_map/pallas_call | solution.py:325
  223.5 2.3 all-to-all-done.7
  225.8 0.0 copy-start
  225.8 1.0 copy-done
  226.8 29.3 %shard_map.194 = f32[32,4,128,128]{3,2,1,0:T(8,128)} custom-call(f32[2048,128]{1,0:T(8,128)} %bitcast.13, f32[32,4,128,128]{3,2,1,0:T(8,128)} %get-tuple-element.5.grad_ref, f32[32,32]{1,0:T(8,128)} %pw_ref.3, f32[256,32]{1,0:T(8,128)} %constant.34.clone.ex_ref, bf16[256,64]{1,0:T(8,128)(2,1)} %constant.35.clone.iy_h, bf16[256,64]{1,0:T(8,128)(2,1)} %constant.36.clone.iy_l, ...), custom_call_target="tpu_custom_call" | custom-call | tf_op jit(solution)/shard_map/pallas_call | solution.py:468
Async XLA Ops:
  46.2 18.3 %all-to-all-start.1 = ((f32[4,8,2,8,128]{4,3,2,1,0:T(8,128)}), f32[4,8,2,8,128]{4,3,2,1,0:T(8,128)S(1)}, u32[]{:S(2)}, u32[]{:S(2)}) async-start(f32[4,8,2,8,128]{4,3,2,1,0:T(8,128)} %shard_map.186), calls=%async_computation.1 | async-start | bytes 524288 | tf_op jit(solution)/shard_map/all_to_all | solution.py:487
  51.8 51.1 %copy-start.2 = (f32[32]{0:T(128)S(1)}, f32[32]{0:T(128)}, u32[]{:S(2)}) copy-start(f32[32]{0:T(128)} %param.22) | copy-start | bytes 388
  64.6 0.7 copy-start.1
  204.9 20.9 %all-to-all-start.7 = ((f32[32,8,8,128]{3,2,1,0:T(8,128)}), f32[32,8,8,128]{3,2,1,0:T(8,128)S(1)}, u32[]{:S(2)}, u32[]{:S(2)}) async-start(f32[32,8,8,128]{3,2,1,0:T(8,128)} %shard_map.193), calls=%async_computation.7 | async-start | bytes 2097152 | tf_op jit(solution)/shard_map/all_to_all | solution.py:487
  225.8 1.0 copy-start

commit v2 on v0

v2 whole, which is shorter than its diff:
```python
from functools import partial

import jax
import jax.numpy as jnp
import ml_dtypes
import numpy as np
from jax import lax
from jax.experimental import pallas as pl
from jax.experimental.pallas import tpu as pltpu
from jax.sharding import PartitionSpec as P

N = 128
M = 32
C = 32
XL = 4
CG = 8
DP = 4
MP = 32
F32 = jnp.float32
BF16 = jnp.bfloat16
VMEM_LIMIT = 60 * 1024 * 1024


def split_np(table):
    table = table.astype(np.float32)
    high = table.astype(ml_dtypes.bfloat16)
    low = (table - high.astype(np.float32)).astype(ml_dtypes.bfloat16)
    return high, low


def angles(signed):
    frequency = np.arange(M)
    if signed:
        frequency = np.where(frequency < M // 2, frequency, frequency - M)
    phase = (np.arange(N)[:, None] * frequency[None, :]) % N
    theta = phase * (2.0 * np.pi / N)
    return np.cos(theta), np.sin(theta)


def make_tables():
    cz, sz = angles(False)
    cs, ss = angles(True)
    tz = np.zeros((4, N, 2, 4, M))
    for c in range(4):
        tz[c, :, 0, c, :] = cz
        tz[c, :, 1, c, :] = sz
    tz = tz.reshape(4 * N, 8 * M)
    ty = np.block([[cs.T, -ss.T], [-ss.T, -cs.T]])
    tx = np.zeros((2, M, N, 2))
    tx[0, :, :, 0] = cs.T
    tx[0, :, :, 1] = ss.T
    tx[1, :, :, 0] = -ss.T
    tx[1, :, :, 1] = cs.T
    tx = tx.reshape(2 * M, 2 * N)
    ix = np.zeros((N, 2, 2, M))
    ix[:, 0, 0] = cs
    ix[:, 0, 1] = -ss
    ix[:, 1, 0] = ss
    ix[:, 1, 1] = cs
    ix = ix.reshape(2 * N, 2 * M)
    iy = np.block([[cs, -ss], [ss, cs]])
    iz = np.zeros((2, 4, M, 4, N))
    for c in range(4):
        iz[0, c, :, c, :] = cz.T
        iz[1, c, :, c, :] = -sz.T
    iz = iz.reshape(8 * M, 4 * N)
    expand = np.repeat(np.eye(C), 8, axis=0)
    return {
        "tz": split_np(tz),
        "ty": split_np(ty),
        "tx": split_np(tx),
        "ix": split_np(ix),
        "iy": split_np(iy),
        "iz": split_np(iz),
        "expand": expand.astype(np.float32),
    }


TABLES = make_tables()


def thrice(pair, axis):
    high, low = pair
    return np.concatenate([high, high, low], axis=axis)


TZ = thrice(TABLES["tz"], 0)
TY = np.concatenate(TABLES["ty"], axis=0)
TX = np.concatenate(TABLES["tx"], axis=0)
IX = thrice(TABLES["ix"], 1)
IY = thrice(TABLES["iy"], 1)
IZ = thrice(TABLES["iz"], 0)
EXPAND = TABLES["expand"]


def split(value):
    high = value.astype(BF16)
    low = (value - high.astype(F32)).astype(BF16)
    return high, low


def mm(a, b):
    return jnp.dot(a, b, preferred_element_type=F32)


def whole(shape):
    return pl.BlockSpec(shape, lambda *_: (0,) * len(shape))


NQ = 4
GQ = CG // NQ
RQ = 8 * GQ
MESH = pl.DeviceIdType.MESH


def position():
    return lax.axis_index("dp"), lax.axis_index("mp")


def greet():
    dp, mp = position()
    barrier = pltpu.get_barrier_semaphore()

    @pl.loop(1, MP)
    def _(k):
        pl.semaphore_signal(
            barrier, inc=1, device_id=(dp, lax.rem(mp + k, MP)), device_id_type=MESH
        )

    for k in range(1, DP):
        pl.semaphore_signal(
            barrier, inc=1, device_id=(lax.rem(dp + k, DP), mp), device_id_type=MESH
        )


def await_greetings():
    pl.semaphore_wait(pltpu.get_barrier_semaphore(), MP - 1 + DP - 1)


def flat_rows(device, q):
    return pl.ds(pl.multiple_of(device * 64 + q * RQ, 8), RQ)


def piece_rows(q):
    return pl.ds(pl.multiple_of(q * RQ, 8), RQ)


def send_to_modes(q, flat, pieces, send_sem, recv_sem):
    dp, mp = position()

    @pl.loop(1, MP)
    def _(k):
        peer = lax.rem(mp + k, MP)
        pltpu.make_async_remote_copy(
            src_ref=flat.at[flat_rows(peer, q)],
            dst_ref=pieces.at[mp, piece_rows(q)],
            send_sem=send_sem.at[q],
            recv_sem=recv_sem.at[q],
            device_id=(dp, peer),
            device_id_type=MESH,
        ).start()


def send_to_cells(q, pieces, flat, send_sem, recv_sem):
    dp, mp = position()

    @pl.loop(1, MP)
    def _(k):
        peer = lax.rem(mp + k, MP)
        pltpu.make_async_remote_copy(
            src_ref=pieces.at[peer, piece_rows(q)],
            dst_ref=flat.at[flat_rows(mp, q)],
            send_sem=send_sem.at[q],
            recv_sem=recv_sem.at[q],
            device_id=(dp, peer),
            device_id_type=MESH,
        ).start()


def drain_mp(q, flat, sem):
    part = flat.at[pl.ds(0, (MP - 1) * RQ)]
    pltpu.make_async_copy(part, part, sem.at[q]).wait()


def send_dp(q, src, dst, send_sem, recv_sem):
    dp, mp = position()
    groups = pl.ds(q * GQ, GQ)
    for k in range(1, DP):
        peer = lax.rem(dp + k, DP)
        pltpu.make_async_remote_copy(
            src_ref=src.at[peer, groups],
            dst_ref=dst.at[dp, groups],
            send_sem=send_sem.at[q],
            recv_sem=recv_sem.at[q],
            device_id=(peer, mp),
            device_id_type=MESH,
        ).start()


def keep_dp(q, src, dst):
    dp, _ = position()
    groups = pl.ds(q * GQ, GQ)
    dst[dp, groups] = src[dp, groups]


def drain_dp(q, ref, sem):
    part = ref.at[pl.ds(0, DP - 1), pl.ds(0, GQ)]
    pltpu.make_async_copy(part, part, sem.at[q]).wait()


def chunks(body):
    @pl.loop(0, NQ)
    def _(q):
        body(q)


def groups_of(q, body):
    @pl.loop(0, GQ)
    def _(h):
        body(q * GQ + h)


def forward_group(field_ref, g, tz, ty, flat):
    rows = jnp.concatenate([field_ref[4 * g + c].reshape(XL * N, N) for c in range(4)], axis=1)
    high, low = split(rows)
    along_z = mm(jnp.concatenate([high, low, high], axis=1), tz[...])
    stacked = jnp.concatenate(
        [
            jnp.concatenate(
                [along_z[x * N : (x + 1) * N, :N], along_z[x * N : (x + 1) * N, N:]], axis=0
            )
            for x in range(XL)
        ],
        axis=1,
    )
    high, low = split(stacked)
    tables = ty[...]
    both = mm(tables, high)
    tile = both[: 2 * M] + both[2 * M :] + mm(tables[: 2 * M], low)
    for x in range(XL):
        for r in range(2):
            flat[pl.ds(g * 8 + 2 * x + r, M, stride=64), :] = tile[
                r * M : (r + 1) * M, x * N : (x + 1) * N
            ]


def inverse_group(flat, g, iy, iz):
    modes = jnp.concatenate(
        [
            jnp.concatenate(
                [flat[pl.ds(g * 8 + 2 * x + r, M, stride=64), :] for r in range(2)], axis=0
            )
            for x in range(XL)
        ],
        axis=1,
    )
    high, low = split(modes)
    along_y = mm(iy[...], jnp.concatenate([high, low, high], axis=0))
    rows = jnp.concatenate(
        [
            jnp.concatenate(
                [along_y[:N, x * N : (x + 1) * N], along_y[N:, x * N : (x + 1) * N]], axis=1
            )
            for x in range(XL)
        ],
        axis=0,
    )
    high, low = split(rows)
    return mm(jnp.concatenate([high, low, high], axis=1), iz[...])


def forward_x(pieces, g, tx, out):
    data = pieces[:, pl.ds(pl.multiple_of(g * 8, 8), 8), :].reshape(2 * N, N)
    high, low = split(data)
    tables = tx[...]
    both = mm(tables, high)
    tile = both[: 2 * M] + both[2 * M :] + mm(tables[: 2 * M], low)
    for d in range(DP):
        for r in range(2):
            out[d, g, r] = tile[r * M + 8 * d : r * M + 8 * d + 8]


def inverse_x(modes, g, ix, pieces):
    rows = jnp.concatenate([modes[:, g, 0].reshape(M, N), modes[:, g, 1].reshape(M, N)], axis=0)
    high, low = split(rows)
    tile = mm(ix[...], jnp.concatenate([high, low, high], axis=0))
    pieces[:, pl.ds(pl.multiple_of(g * 8, 8), 8), :] = tile.reshape(MP, 8, N)


def channel_matrix(matrix, expand, mat):
    spread_cols = lax.dot_general(
        matrix, expand, (((1,), (1,)), ((), ())), precision=lax.Precision.HIGHEST
    )
    full = jnp.dot(expand, spread_cols, precision=lax.Precision.HIGHEST)
    row = lax.broadcasted_iota(jnp.int32, (8 * C, 8 * C), 0)
    col = lax.broadcasted_iota(jnp.int32, (8 * C, 8 * C), 1)
    high, low = split(jnp.where(row % 8 == col % 8, full, 0.0))
    mat[: 8 * C] = high
    mat[8 * C :] = low


YB = 4


def channel_map(in_ref, x, mat, out_ref):
    @pl.loop(0, N // (8 * YB))
    def _(t):
        y = pl.multiple_of(t * 8 * YB, 8)
        data = jnp.concatenate(
            [in_ref[:, x, pl.ds(y + 8 * h, 8), :].reshape(8 * C, N) for h in range(YB)], axis=1
        )
        high, low = split(data)
        tables = mat[...]
        both = mm(tables, high)
        mapped = both[: 8 * C] + both[8 * C :] + mm(tables[: 8 * C], low)
        for h in range(YB):
            out_ref[:, x, pl.ds(y + 8 * h, 8), :] = mapped[:, h * N : (h + 1) * N].reshape(C, 8, N)


def factor_lanes():
    lane = lax.broadcasted_iota(jnp.int32, (8, N), 1)
    return jnp.where(lane % M == 0, 1.0, 2.0).astype(F32) * (1.0 / float(N * N * N))


def lane_groups():
    return lax.broadcasted_iota(jnp.int32, (8, N), 1) // M


def pick(groups, tiles):
    low = jnp.where(groups == 0, tiles[0], tiles[1])
    high = jnp.where(groups == 2, tiles[2], tiles[3])
    return jnp.where(groups < 2, low, high)


def mix(spec_ref, w_ref, g, out_ref):
    groups = lane_groups()
    factor = factor_lanes()
    totals = [[[] for _ in range(2)] for _ in range(DP)]
    for q in range(4):
        o = 4 * g + q
        acc = [[None, None] for _ in range(DP)]
        for i in range(CG):
            wr, wi = w_ref[0, i, o], w_ref[1, i, o]
            for b in range(DP):
                sr, si = spec_ref[b, i, 0], spec_ref[b, i, 1]
                re = wr * sr - wi * si
                im = wr * si + wi * sr
                acc[b] = [re, im] if i == 0 else [acc[b][0] + re, acc[b][1] + im]
        for b in range(DP):
            for r in range(2):
                v = acc[b][r]
                v = v + pltpu.roll(v, 64, 1)
                totals[b][r].append(v + pltpu.roll(v, 32, 1))
    for b in range(DP):
        for r in range(2):
            out_ref[b, g, r] = pick(groups, totals[b][r]) * factor


def spread(grad_ref, rep_ref):
    groups = lane_groups()
    factor = factor_lanes()

    @pl.loop(0, CG)
    def _(g):
        for b in range(DP):
            for r in range(2):
                v = grad_ref[b, g, r] * factor
                rolled = [v] + [pltpu.roll(v, M * s, 1) for s in range(1, 4)]
                for q in range(4):
                    rep_ref[4 * g + q, b, r] = pick(
                        groups, [rolled[(h - q) % 4] for h in range(4)]
                    )


def back_mix(rep_ref, w_ref, i, out_ref):
    def step(t, acc):
        acc = list(acc)
        for u in range(4):
            o = 4 * t + u
            wr, wi = w_ref[0, i, o], w_ref[1, i, o]
            for b in range(DP):
                gr, gi = rep_ref[o, b, 0], rep_ref[o, b, 1]
                acc[2 * b] = acc[2 * b] + (wr * gr + wi * gi)
                acc[2 * b + 1] = acc[2 * b + 1] + (wr * gi - wi * gr)
        return tuple(acc)

    acc = lax.fori_loop(0, 8, step, tuple(jnp.zeros((8, N), F32) for _ in range(8)))
    for b in range(DP):
        for r in range(2):
            out_ref[b, i, r] = acc[2 * b + r]


def weight_grad(rep_ref, spec_ref, o, out_ref):
    grads = [[rep_ref[o, b, r] for r in range(2)] for b in range(DP)]
    for i in range(CG):
        re = im = None
        for b in range(DP):
            gr, gi = grads[b]
            sr, si = spec_ref[b, i, 0], spec_ref[b, i, 1]
            r1 = gr * sr + gi * si
            i1 = gi * sr - gr * si
            re, im = (r1, i1) if b == 0 else (re + r1, im + i1)
        out_ref[0, i, o] = re
        out_ref[1, i, o] = im


def params(collective_id=None):
    if collective_id is None:
        return pltpu.CompilerParams(vmem_limit_bytes=VMEM_LIMIT)
    return pltpu.CompilerParams(
        vmem_limit_bytes=VMEM_LIMIT, collective_id=collective_id, has_side_effects=True
    )


def in_vmem():
    return pl.BlockSpec(memory_space=pltpu.VMEM)


def anywhere():
    return pl.BlockSpec(memory_space=pl.ANY)


def sems(count):
    return pltpu.SemaphoreType.DMA((count,))


SPEC = (DP, CG, 2, 8, N)
FLAT = (M * 64, N)
PIECES = (MP, 64, N)
CELLS = (C, XL, N, N)
PACKED = (2, CG, C, 8, N)


def to_spectrum(flat, pieces, held, out, tx, mp_sems, dp_sems):
    _, mp = position()

    def body(q):
        drain_mp(q, flat, mp_sems[1])
        pieces[mp, piece_rows(q)] = flat[flat_rows(mp, q)]
        groups_of(q, lambda g: forward_x(pieces, g, tx, held))
        send_dp(q, held, out, *dp_sems)
        keep_dp(q, held, out)

    chunks(body)


def start_kernel(
    field_ref, w_ref, tz, ty, tx, spec_ref, packed_ref,
    fields, weight, flat, pieces, held, landed,
    field_sem, weight_sem, mp_send, mp_recv, dp_send, dp_recv,
):
    greet()

    def field_copy(g):
        part = pl.ds(4 * g, 4)
        return pltpu.make_async_copy(field_ref.at[part], fields.at[part], field_sem.at[g])

    @pl.loop(0, CG)
    def _(g):
        field_copy(g).start()

    weight_copy = pltpu.make_async_copy(w_ref, weight, weight_sem.at[0])
    weight_copy.start()

    def transform(g):
        field_copy(g).wait()
        forward_group(fields, g, tz, ty, flat)

    def body(q):
        groups_of(q, transform)

        @pl.when(q == 0)
        def _():
            await_greetings()

        send_to_modes(q, flat, pieces, mp_send, mp_recv)

    chunks(body)
    weight_copy.wait()

    @pl.loop(0, C)
    def _(o):
        for r in range(2):
            for g in range(CG):
                packed_ref[r, g, o] = jnp.concatenate(
                    [weight[r, 4 * g + q, o] for q in range(4)], axis=1
                )

    to_spectrum(flat, pieces, held, landed, tx, (mp_send, mp_recv), (dp_send, dp_recv))
    chunks(lambda q: drain_dp(q, landed, dp_recv))
    spec_ref[...] = landed[...]
    chunks(lambda q: drain_mp(q, flat, mp_send))
    chunks(lambda q: drain_dp(q, landed, dp_send))


def start(fields, weight):
    tabs = [TZ, TY, TX]
    return pl.pallas_call(
        start_kernel,
        in_specs=[anywhere(), anywhere()] + [in_vmem()] * len(tabs),
        out_specs=[in_vmem(), in_vmem()],
        out_shape=[jax.ShapeDtypeStruct(SPEC, F32), jax.ShapeDtypeStruct(PACKED, F32)],
        scratch_shapes=[
            pltpu.VMEM(CELLS, F32),
            pltpu.VMEM((2, C, C, 8, M), F32),
            pltpu.VMEM(FLAT, F32),
            pltpu.VMEM(PIECES, F32),
            pltpu.VMEM(SPEC, F32),
            pltpu.VMEM(SPEC, F32),
            sems(CG),
            sems(1),
        ]
        + [sems(NQ)] * 4,
        compiler_params=params(1),
    )(fields, weight, *map(jnp.asarray, tabs))


def plane_copy(src, dst, sem, x):
    return pltpu.make_async_copy(src.at[:, x], dst.at[:, x], sem.at[x])


def to_planes(modes, pieces, flat, ix, mp_sems, dp_recv):
    def body(q):
        drain_dp(q, modes, dp_recv)
        groups_of(q, lambda g: inverse_x(modes, g, ix, pieces))
        send_to_cells(q, pieces, flat, *mp_sems)

    chunks(body)


def middle_kernel(
    spec_ref, packed_ref, field_ref, up_ref, pw_ref, bias_ref, ex_ref, ix, iy, iz, tz, ty, tx,
    spec_out, grad_out,
    fields, upstream, cells, mat, mixed, modes, ipieces, iflat, flat, pieces, held, landed,
    field_sem, up_sem, grad_sem,
    d1_send, d1_recv, m1_send, m1_recv, m2_send, m2_recv, d2_send, d2_recv,
):
    _, mp = position()
    greet()
    for x in range(XL):
        plane_copy(field_ref, fields, field_sem, x).start()
    up_copy = pltpu.make_async_copy(up_ref, upstream, up_sem.at[0])
    up_copy.start()

    def mix_chunk(q):
        groups_of(q, lambda g: mix(spec_ref, packed_ref, g, mixed))

        @pl.when(q == 0)
        def _():
            await_greetings()

        send_dp(q, mixed, modes, d1_send, d1_recv)
        keep_dp(q, mixed, modes)

    chunks(mix_chunk)
    channel_matrix(pw_ref[...].T, ex_ref[...], mat)

    def point(x):
        plane_copy(field_ref, fields, field_sem, x).wait()
        channel_map(fields, x, mat, cells)

    to_planes(modes, ipieces, iflat, ix, (m1_send, m1_recv), d1_recv)

    @pl.loop(0, XL)
    def _(x):
        point(x)

    up_copy.wait()

    def cell_group(g):
        spectral = inverse_group(iflat, g, iy, iz)
        for c in range(4):
            cells[4 * g + c] = (
                cells[4 * g + c]
                + spectral[:, c * N : (c + 1) * N].reshape(XL, N, N)
                + bias_ref[4 * g + c]
            )

        @pl.loop(0, 4 * XL)
        def _(t):
            o, x = 4 * g + t // XL, t % XL
            pre = cells[o, x]
            cdf = 0.5 * (1.0 + lax.erf(pre * np.float32(np.sqrt(0.5))))
            density = jnp.exp(-0.5 * pre * pre) * np.float32(1 / np.sqrt(2 * np.pi))
            cells[o, x] = upstream[o, x].astype(F32) * (cdf + pre * density)

        forward_group(cells, g, tz, ty, flat)

    def grad_copy(q):
        part = pl.ds(q * 4 * GQ, 4 * GQ)
        return pltpu.make_async_copy(cells.at[part], grad_out.at[part], grad_sem.at[q])

    def cell_chunk(q):
        drain_mp(q, iflat, m1_recv)
        iflat[flat_rows(mp, q)] = ipieces[mp, piece_rows(q)]
        groups_of(q, cell_group)
        send_to_modes(q, flat, pieces, m2_send, m2_recv)
        grad_copy(q).start()

    chunks(cell_chunk)
    to_spectrum(flat, pieces, held, landed, tx, (m2_send, m2_recv), (d2_send, d2_recv))
    chunks(lambda q: drain_dp(q, landed, d2_recv))
    spec_out[...] = landed[...]
    chunks(lambda q: drain_dp(q, landed, d1_send))
    chunks(lambda q: drain_dp(q, landed, d2_send))
    chunks(lambda q: drain_mp(q, flat, m1_send))
    chunks(lambda q: drain_mp(q, flat, m2_send))
    chunks(lambda q: grad_copy(q).wait())


def middle(spectrum, packed, fields, upstream, point_weight, point_bias):
    tabs = [IX, IY, IZ, TZ, TY, TX]
    return pl.pallas_call(
        middle_kernel,
        in_specs=[in_vmem(), in_vmem(), anywhere(), anywhere()] + [in_vmem()] * (3 + len(tabs)),
        out_specs=[in_vmem(), anywhere()],
        out_shape=[jax.ShapeDtypeStruct(SPEC, F32), jax.ShapeDtypeStruct(CELLS, F32)],
        scratch_shapes=[
            pltpu.VMEM(CELLS, F32),
            pltpu.VMEM(CELLS, BF16),
            pltpu.VMEM(CELLS, F32),
            pltpu.VMEM((16 * C, 8 * C), BF16),
            pltpu.VMEM(SPEC, F32),
            pltpu.VMEM(SPEC, F32),
            pltpu.VMEM(PIECES, F32),
            pltpu.VMEM(FLAT, F32),
            pltpu.VMEM(FLAT, F32),
            pltpu.VMEM(PIECES, F32),
            pltpu.VMEM(SPEC, F32),
            pltpu.VMEM(SPEC, F32),
            sems(XL),
            sems(1),
            sems(NQ),
        ]
        + [sems(NQ)] * 8,
        compiler_params=params(2),
    )(
        spectrum,
        packed,
        fields,
        upstream,
        point_weight,
        jnp.broadcast_to(point_bias[:, None, None], (C, 1, N)),
        jnp.asarray(EXPAND),
        *map(jnp.asarray, tabs),
    )


def back_kernel(
    grad_spec, spec_ref, packed_ref, grad_ref, pw_ref, ex_ref, ix,
    flat_out, wgrad_out, point_out,
    rep, grads, point, mat, mixed, modes, pieces, flat,
    grad_sem, point_sem, d_send, d_recv, m_send, m_recv,
):
    _, mp = position()
    greet()
    for x in range(XL):
        plane_copy(grad_ref, grads, grad_sem, x).start()
    spread(grad_spec, rep)

    def mix_chunk(q):
        groups_of(q, lambda i: back_mix(rep, packed_ref, i, mixed))

        @pl.when(q == 0)
        def _():
            await_greetings()

        send_dp(q, mixed, modes, d_send, d_recv)
        keep_dp(q, mixed, modes)

    chunks(mix_chunk)
    channel_matrix(pw_ref[...], ex_ref[...], mat)
    to_planes(modes, pieces, flat, ix, (m_send, m_recv), d_recv)

    @pl.loop(0, C)
    def _(o):
        weight_grad(rep, spec_ref, o, wgrad_out)

    @pl.loop(0, XL)
    def _(x):
        plane_copy(grad_ref, grads, grad_sem, x).wait()
        channel_map(grads, x, mat, point)
        plane_copy(point, point_out, point_sem, x).start()

    def land(q):
        drain_mp(q, flat, m_recv)
        flat[flat_rows(mp, q)] = pieces[mp, piece_rows(q)]

    chunks(land)
    flat_out[...] = flat[...]
    chunks(lambda q: drain_dp(q, modes, d_send))
    chunks(lambda q: drain_mp(q, flat, m_send))
    for x in range(XL):
        plane_copy(point, point_out, point_sem, x).wait()


def back(grad_spec, spectrum, packed, grad_pre, point_weight):
    return pl.pallas_call(
        back_kernel,
        in_specs=[in_vmem(), in_vmem(), in_vmem(), anywhere(), in_vmem(), in_vmem(), in_vmem()],
        out_specs=[in_vmem(), in_vmem(), anywhere()],
        out_shape=[
            jax.ShapeDtypeStruct(FLAT, F32),
            jax.ShapeDtypeStruct(PACKED, F32),
            jax.ShapeDtypeStruct(CELLS, F32),
        ],
        scratch_shapes=[
            pltpu.VMEM((C, DP, 2, 8, N), F32),
            pltpu.VMEM(CELLS, F32),
            pltpu.VMEM(CELLS, F32),
            pltpu.VMEM((16 * C, 8 * C), BF16),
            pltpu.VMEM(SPEC, F32),
            pltpu.VMEM(SPEC, F32),
            pltpu.VMEM(PIECES, F32),
            pltpu.VMEM(FLAT, F32),
            sems(XL),
            sems(XL),
        ]
        + [sems(NQ)] * 4,
        compiler_params=params(3),
    )(grad_spec, spectrum, packed, grad_pre, point_weight, jnp.asarray(EXPAND), jnp.asarray(IX))


def finish_kernel(flat, point, wgrad, iy, iz, cells_out, wgrad_out):
    g = pl.program_id(0)
    spectral = inverse_group(flat, g, iy, iz)
    for c in range(4):
        cells_out[c] = point[c] + spectral[:, c * N : (c + 1) * N].reshape(XL, N, N)

    @pl.loop(0, C // 4)
    def _(t):
        for u in range(4):
            for r in range(2):
                tile = wgrad[r, t * 4 + u]
                for q in range(4):
                    wgrad_out[r, q, t * 4 + u] = tile[:, M * q : M * (q + 1)]


def finish(flat, point, wgrad):
    cell_spec = pl.BlockSpec((4, XL, N, N), lambda g: (g, 0, 0, 0))
    return pl.pallas_call(
        finish_kernel,
        grid=(CG,),
        in_specs=[
            whole(FLAT),
            cell_spec,
            pl.BlockSpec((2, pl.Squeezed(), C, 8, N), lambda g: (0, g, 0, 0, 0)),
            whole(IY.shape),
            whole(IZ.shape),
        ],
        out_specs=[cell_spec, pl.BlockSpec((2, 4, C, 8, M), lambda g: (0, g, 0, 0, 0))],
        out_shape=[
            jax.ShapeDtypeStruct(CELLS, F32),
            jax.ShapeDtypeStruct((2, C, C, 8, M), F32),
        ],
        compiler_params=params(),
    )(flat, point, wgrad, jnp.asarray(IY), jnp.asarray(IZ))


def shards(fields, upstream, spectral_weight, point_weight, point_bias):
    fields = fields[0]
    spectrum, packed = start(fields, spectral_weight)
    grad_spec, grad_pre = middle(
        spectrum, packed, fields, upstream[0], point_weight, point_bias
    )
    flat, wgrad, point = back(grad_spec, spectrum, packed, grad_pre, point_weight)
    grad_fields, weight_out = finish(flat, point, wgrad)
    return (grad_fields[None], weight_out)


def solution(mesh):
    placed = (
        P("dp", None, "mp", None, None),
        P("dp", None, "mp", None, None),
        P(None, None, None, "dp", "mp"),
        P(),
        P(),
    )
    return jax.shard_map(
        shards,
        mesh=mesh,
        in_specs=placed,
        out_specs=(P("dp", None, "mp", None, None), P(None, None, None, "dp", "mp")),
        check_vma=False,
    )
```

time: 857 us -> 133 us (0.16)
  waiting for transfers between devices: 422 us -> 0 us
  matrix products: 131 us -> 0 us
  Pallas kernels: 0 us -> 130 us
  local copies, waits for them, and re-layouts: 131 us -> 1.36 us
  other arithmetic: 97.4 us -> 0 us
  starting transfers between devices: 26.2 us -> 0 us
  blocking collectives: 26 us -> 0 us
  between operations: 15 us -> 0.65 us
    all_gather x1 -> x0, waiting for transfers between devices: 215 us -> none  [shards(): full_weight = lax.all_gather(spectral_weight, 'dp', axis=3, tiled=True)]
    reduce_scatter x1 -> x0, waiting for transfers between devices: 188 us -> none  [shards(): lax.psum_scatter(weight_gradient(grad_spec, spectrum), 'dp', scatter_dime...]
    pallas_call x0 -> x4, Pallas kernels: none -> 130 us  [the longest x1 55.9 us: middle(): pl.pallas_call(middle_kernel, in_specs=[in_vmem(), in_vmem(), anywhere(),...]
    dot_general x12 -> x0, matrix products: 129 us -> none  [the longest x2 67.3 us: inverse_plane(): return jnp.einsum('scpyj,zj->scpyz', merged, table_z, precision=HIGHEST)]
    unnamed x29 -> x0, local copies, waits for them, and re-layouts: 49.8 us -> none
    unnamed x7 -> x0, other arithmetic: 48.2 us -> none
    all_to_all x7 -> x0, local copies, waits for them, and re-layouts: 44.5 us -> none  [the longest x3 14.6 us: shards(): lax.all_to_all(forward_plane(fields, table_y, table_z), 'mp', split_axis=...]
    all_to_all x3 -> x0, starting transfers between devices: 26.1 us -> none  [the longest x1 11.3 us: shards(): lax.all_to_all(forward_plane(fields, table_y, table_z), 'mp', split_axis=...]
  transfers between devices with their start and end apart: 5 -> 0, of which waited for: 4 -> 0; matrix products, arithmetic and copies ran while one was open for 21% -> 0% of each run, Pallas kernels for 0% -> 0%
where the time goes in v2:
time: 133 us; the launch traced here: 132 us
  Pallas kernels  130 us (98%)
  local copies, waits for them, and re-layouts  1.36 us (1%)
    pallas_call x1, Pallas kernels, middle(): pl.pallas_call(middle_kernel, in_specs=[in_vmem(), in_vmem(), anywhere(),...  55.9 us
    pallas_call x1, Pallas kernels, start(): pl.pallas_call(start_kernel, in_specs=[anywhere(), anywhere()] + [in_vmem...  30 us
    pallas_call x1, Pallas kernels, back(): pl.pallas_call(back_kernel, in_specs=[in_vmem(), in_vmem(), in_vmem(), an...  27.3 us
    pallas_call x1, Pallas kernels, finish(): pl.pallas_call(finish_kernel, grid=(CG,), in_specs=[whole(FLAT), cell_spe...  17.1 us

profile of v2, /device:TPU:1, one launch (start us, length us, event | category | flops | bytes accessed | tf_op | source)
XLA Modules:
  0.0 132.4 jit_solution(5057085648405116935)
XLA Ops:
  0.6 1.4 %broadcast_in_dim.4.bias_ref = f32[32,1,128]{2,1,0:T(1,128)} broadcast(f32[32]{0:T(128)} %param.16), dimensions={0} | broadcast | bytes 16512 | tf_op jit(solution)/shard_map/broadcast_in_dim | solution.py:643
  2.0 30.0 %shard_map.131 = (f32[4,8,2,8,128]{4,3,2,1,0:T(8,128)}, f32[2,8,32,8,128]{4,3,2,1,0:T(8,128)}) custom-call(f32[32,4,128,128]{3,2,1,0:T(8,128)} %bitcast.3, f32[2,32,32,8,32]{4,3,2,1,0:T(8,128)} %w_ref.1, bf16[1536,256]{1,0:T(8,128)(2,1)} %constant.14.clone.tz, bf16[128,256]{1,0:T(8,128)(2,1)} %constant.15.clone.ty, bf16[128,256]{1,0:T(8,128)(2,1)} %constant.16.clone.tx), custom_call_target="tpu_custom_call" | custom-call | tf_op jit(solution)/shard_map/pallas_call | solution.py:498
  32.0 55.9 %shard_map.132 = (f32[4,8,2,8,128]{4,3,2,1,0:T(8,128)}, f32[32,4,128,128]{3,2,1,0:T(8,128)}) custom-call(f32[4,8,2,8,128]{4,3,2,1,0:T(8,128)} %get-tuple-element.11.spec_ref, f32[2,8,32,8,128]{4,3,2,1,0:T(8,128)} %get-tuple-element.12.packed_ref, f32[32,4,128,128]{3,2,1,0:T(8,128)} %bitcast.4, bf16[32,4,128,128]{3,2,1,0:T(8,128)(2,1)} %bitcast.5, ...), custom_call_target="tpu_custom_call" | custom-call | tf_op jit(solution)/shard_map/pallas_call | solution.py:613
  87.9 27.3 %shard_map.133 = (f32[2048,128]{1,0:T(8,128)}, f32[2,8,32,8,128]{4,3,2,1,0:T(8,128)}, f32[32,4,128,128]{3,2,1,0:T(8,128)}) custom-call(f32[4,8,2,8,128]{4,3,2,1,0:T(8,128)} %get-tuple-element.13.grad_spec, f32[4,8,2,8,128]{4,3,2,1,0:T(8,128)} %get-tuple-element.11.spec_ref, f32[2,8,32,8,128]{4,3,2,1,0:T(8,128)} %get-tuple-element.12.packed_ref, ...), custom_call_target="tpu_custom_call" | custom-call | tf_op jit(solution)/shard_map/pallas_call | solution.py:698
  115.2 17.1 %shard_map.134 = (f32[32,4,128,128]{3,2,1,0:T(8,128)}, f32[2,32,32,8,32]{4,3,2,1,0:T(8,128)}) custom-call(f32[2048,128]{1,0:T(8,128)} %get-tuple-element.15.flat, f32[32,4,128,128]{3,2,1,0:T(8,128)} %get-tuple-element.16.point, f32[2,8,32,8,128]{4,3,2,1,0:T(8,128)} %get-tuple-element.17.wgrad, bf16[256,192]{1,0:T(8,128)(2,1)} %constant.19.clone.iy, ...), custom_call_target="tpu_custom_call" | custom-call | tf_op jit(solution)/shard_map/pallas_call | solution.py:741

commit v3 on v2

v3 whole, which is shorter than its diff:
```python
from functools import partial

import jax
import jax.numpy as jnp
import ml_dtypes
import numpy as np
from jax import lax
from jax.experimental import pallas as pl
from jax.experimental.pallas import tpu as pltpu
from jax.sharding import PartitionSpec as P

N = 128
M = 32
C = 32
XL = 4
CG = 8
DP = 4
MP = 32
F32 = jnp.float32
BF16 = jnp.bfloat16
VMEM_LIMIT = 60 * 1024 * 1024


def split_np(table):
    table = table.astype(np.float32)
    high = table.astype(ml_dtypes.bfloat16)
    low = (table - high.astype(np.float32)).astype(ml_dtypes.bfloat16)
    return high, low


def angles(signed):
    frequency = np.arange(M)
    if signed:
        frequency = np.where(frequency < M // 2, frequency, frequency - M)
    phase = (np.arange(N)[:, None] * frequency[None, :]) % N
    theta = phase * (2.0 * np.pi / N)
    return np.cos(theta), np.sin(theta)


def make_tables():
    cz, sz = angles(False)
    cs, ss = angles(True)
    tz = np.zeros((4, N, 2, 4, M))
    for c in range(4):
        tz[c, :, 0, c, :] = cz
        tz[c, :, 1, c, :] = sz
    tz = tz.reshape(4 * N, 8 * M)
    ty = np.block([[cs.T, -ss.T], [-ss.T, -cs.T]])
    tx = np.zeros((2, M, N, 2))
    tx[0, :, :, 0] = cs.T
    tx[0, :, :, 1] = ss.T
    tx[1, :, :, 0] = -ss.T
    tx[1, :, :, 1] = cs.T
    tx = tx.reshape(2 * M, 2 * N)
    ix = np.zeros((N, 2, 2, M))
    ix[:, 0, 0] = cs
    ix[:, 0, 1] = -ss
    ix[:, 1, 0] = ss
    ix[:, 1, 1] = cs
    ix = ix.reshape(2 * N, 2 * M)
    iy = np.block([[cs, -ss], [ss, cs]])
    iz = np.zeros((2, 4, M, 4, N))
    for c in range(4):
        iz[0, c, :, c, :] = cz.T
        iz[1, c, :, c, :] = -sz.T
    iz = iz.reshape(8 * M, 4 * N)
    expand = np.repeat(np.eye(C), 8, axis=0)
    return {
        "tz": split_np(tz),
        "ty": split_np(ty),
        "tx": split_np(tx),
        "ix": split_np(ix),
        "iy": split_np(iy),
        "iz": split_np(iz),
        "expand": expand.astype(np.float32),
    }


TABLES = make_tables()


def thrice(pair, axis):
    high, low = pair
    return np.concatenate([high, high, low], axis=axis)


TZ = thrice(TABLES["tz"], 0)
TY = np.concatenate(TABLES["ty"], axis=0)
TX = np.concatenate(TABLES["tx"], axis=0)
IX = thrice(TABLES["ix"], 1)
IY = thrice(TABLES["iy"], 1)
IZ = thrice(TABLES["iz"], 0)
EXPAND = TABLES["expand"]


def lane_tables():
    eye = np.eye(M)
    pack = np.zeros((4, N, 4, M))
    unpack = np.zeros((4, M, 4, N))
    copy = np.zeros((4, M, 4, 4, M))
    for q in range(4):
        pack[q, :M, q] = eye
        unpack[q, :, q, :M] = eye
        for h in range(4):
            copy[q, :, q, h] = eye
    pack = pack.reshape(4 * N, N)
    unpack = unpack.reshape(N, 4 * N)
    copy = copy.reshape(N, 4 * N)
    gather = copy.T
    tables = [pack, unpack, copy, gather]
    return [np.concatenate([t, t], axis=0).astype(ml_dtypes.bfloat16) for t in tables]


PACK, UNPACK, COPY, GATHER = lane_tables()


def split(value):
    high = value.astype(BF16)
    low = (value - high.astype(F32)).astype(BF16)
    return high, low


def mm(a, b):
    return jnp.dot(a, b, preferred_element_type=F32)


def move_lanes(data, table):
    high, low = split(data)
    return mm(jnp.concatenate([high, low], axis=1), table[...])


def whole(shape):
    return pl.BlockSpec(shape, lambda *_: (0,) * len(shape))


NQ = 4
AHEAD = 2
GQ = CG // NQ
RQ = 8 * GQ
MESH = pl.DeviceIdType.MESH


def position():
    return lax.axis_index("dp"), lax.axis_index("mp")


def greet():
    dp, mp = position()
    barrier = pltpu.get_barrier_semaphore()

    @pl.loop(1, MP)
    def _(k):
        pl.semaphore_signal(
            barrier, inc=1, device_id=(dp, lax.rem(mp + k, MP)), device_id_type=MESH
        )

    for k in range(1, DP):
        pl.semaphore_signal(
            barrier, inc=1, device_id=(lax.rem(dp + k, DP), mp), device_id_type=MESH
        )


def await_greetings():
    pl.semaphore_wait(pltpu.get_barrier_semaphore(), MP - 1 + DP - 1)


def flat_rows(device, q):
    return pl.ds(pl.multiple_of(device * 64 + q * RQ, 8), RQ)


def piece_rows(q):
    return pl.ds(pl.multiple_of(q * RQ, 8), RQ)


def send_to_modes(q, flat, pieces, send_sem, recv_sem):
    dp, mp = position()

    @pl.loop(1, MP)
    def _(k):
        peer = lax.rem(mp + k, MP)
        pltpu.make_async_remote_copy(
            src_ref=flat.at[flat_rows(peer, q)],
            dst_ref=pieces.at[mp, piece_rows(q)],
            send_sem=send_sem.at[q],
            recv_sem=recv_sem.at[q],
            device_id=(dp, peer),
            device_id_type=MESH,
        ).start()


def send_to_cells(q, pieces, flat, send_sem, recv_sem):
    dp, mp = position()

    @pl.loop(1, MP)
    def _(k):
        peer = lax.rem(mp + k, MP)
        pltpu.make_async_remote_copy(
            src_ref=pieces.at[peer, piece_rows(q)],
            dst_ref=flat.at[flat_rows(mp, q)],
            send_sem=send_sem.at[q],
            recv_sem=recv_sem.at[q],
            device_id=(dp, peer),
            device_id_type=MESH,
        ).start()


def drain_mp(q, flat, sem):
    part = flat.at[pl.ds(0, (MP - 1) * RQ)]
    pltpu.make_async_copy(part, part, sem.at[q]).wait()


def send_dp(q, src, dst, send_sem, recv_sem):
    dp, mp = position()
    groups = pl.ds(q * GQ, GQ)
    for k in range(1, DP):
        peer = lax.rem(dp + k, DP)
        pltpu.make_async_remote_copy(
            src_ref=src.at[peer, groups],
            dst_ref=dst.at[dp, groups],
            send_sem=send_sem.at[q],
            recv_sem=recv_sem.at[q],
            device_id=(peer, mp),
            device_id_type=MESH,
        ).start()


def keep_dp(q, src, dst):
    dp, _ = position()
    groups = pl.ds(q * GQ, GQ)
    dst[dp, groups] = src[dp, groups]


def drain_dp(q, ref, sem):
    part = ref.at[pl.ds(0, DP - 1), pl.ds(0, GQ)]
    pltpu.make_async_copy(part, part, sem.at[q]).wait()


def chunks(body):
    @pl.loop(0, NQ)
    def _(q):
        body(q)


def groups_of(q, body):
    @pl.loop(0, GQ)
    def _(h):
        body(q * GQ + h)


def forward_group(field_ref, g, tz, ty, flat):
    rows = jnp.concatenate([field_ref[4 * g + c].reshape(XL * N, N) for c in range(4)], axis=1)
    high, low = split(rows)
    along_z = mm(jnp.concatenate([high, low, high], axis=1), tz[...])
    stacked = jnp.concatenate(
        [
            jnp.concatenate(
                [along_z[x * N : (x + 1) * N, :N], along_z[x * N : (x + 1) * N, N:]], axis=0
            )
            for x in range(XL)
        ],
        axis=1,
    )
    high, low = split(stacked)
    tables = ty[...]
    both = mm(tables, high)
    tile = both[: 2 * M] + both[2 * M :] + mm(tables[: 2 * M], low)
    for x in range(XL):
        for r in range(2):
            flat[pl.ds(g * 8 + 2 * x + r, M, stride=64), :] = tile[
                r * M : (r + 1) * M, x * N : (x + 1) * N
            ]


def inverse_group(flat, g, iy, iz):
    modes = jnp.concatenate(
        [
            jnp.concatenate(
                [flat[pl.ds(g * 8 + 2 * x + r, M, stride=64), :] for r in range(2)], axis=0
            )
            for x in range(XL)
        ],
        axis=1,
    )
    high, low = split(modes)
    along_y = mm(iy[...], jnp.concatenate([high, low, high], axis=0))
    rows = jnp.concatenate(
        [
            jnp.concatenate(
                [along_y[:N, x * N : (x + 1) * N], along_y[N:, x * N : (x + 1) * N]], axis=1
            )
            for x in range(XL)
        ],
        axis=0,
    )
    high, low = split(rows)
    return mm(jnp.concatenate([high, low, high], axis=1), iz[...])


def chunk_rows(q, h):
    return pl.ds(pl.multiple_of((q * GQ + h) * 8, 8), 8)


def forward_x(pieces, q, tx, out):
    data = jnp.concatenate(
        [pieces[:, chunk_rows(q, h), :].reshape(2 * N, N) for h in range(GQ)], axis=1
    )
    high, low = split(data)
    tables = tx[...]
    both = mm(tables, high)
    tile = both[: 2 * M] + both[2 * M :] + mm(tables[: 2 * M], low)
    for h in range(GQ):
        for d in range(DP):
            for r in range(2):
                out[d, q * GQ + h, r] = tile[
                    r * M + 8 * d : r * M + 8 * d + 8, h * N : (h + 1) * N
                ]


def inverse_x(modes, q, ix, pieces):
    rows = jnp.concatenate(
        [
            jnp.concatenate([modes[:, q * GQ + h, r].reshape(M, N) for r in range(2)], axis=0)
            for h in range(GQ)
        ],
        axis=1,
    )
    high, low = split(rows)
    tile = mm(ix[...], jnp.concatenate([high, low, high], axis=0))
    for h in range(GQ):
        pieces[:, chunk_rows(q, h), :] = tile[:, h * N : (h + 1) * N].reshape(MP, 8, N)


def channel_matrix(matrix, expand, mat):
    spread_cols = lax.dot_general(
        matrix, expand, (((1,), (1,)), ((), ())), precision=lax.Precision.HIGHEST
    )
    full = jnp.dot(expand, spread_cols, precision=lax.Precision.HIGHEST)
    row = lax.broadcasted_iota(jnp.int32, (8 * C, 8 * C), 0)
    col = lax.broadcasted_iota(jnp.int32, (8 * C, 8 * C), 1)
    high, low = split(jnp.where(row % 8 == col % 8, full, 0.0))
    mat[: 8 * C] = high
    mat[8 * C :] = low


YB = 8


def channel_map(in_ref, x, mat, out_ref):
    @pl.loop(0, N // (8 * YB))
    def _(t):
        y = pl.multiple_of(t * 8 * YB, 8)
        data = jnp.concatenate(
            [in_ref[:, x, pl.ds(y + 8 * h, 8), :].reshape(8 * C, N) for h in range(YB)], axis=1
        )
        high, low = split(data)
        tables = mat[...]
        both = mm(tables, high)
        mapped = both[: 8 * C] + both[8 * C :] + mm(tables[: 8 * C], low)
        for h in range(YB):
            out_ref[:, x, pl.ds(y + 8 * h, 8), :] = mapped[:, h * N : (h + 1) * N].reshape(C, 8, N)


def factor_lanes():
    lane = lax.broadcasted_iota(jnp.int32, (8, N), 1)
    return jnp.where(lane % M == 0, 1.0, 2.0).astype(F32) * (1.0 / float(N * N * N))


def mix(spec_ref, w_ref, q, gather, sums, out_ref):
    @pl.loop(0, GQ)
    def _(h):
        for c in range(4):
            o = 4 * (q * GQ + h) + c
            acc = [[None, None] for _ in range(DP)]
            for i in range(CG):
                wr, wi = w_ref[0, i, o], w_ref[1, i, o]
                for b in range(DP):
                    sr, si = spec_ref[b, i, 0], spec_ref[b, i, 1]
                    re = wr * sr - wi * si
                    im = wr * si + wi * sr
                    acc[b] = [re, im] if i == 0 else [acc[b][0] + re, acc[b][1] + im]
            for b in range(DP):
                for r in range(2):
                    at = pl.ds(pl.multiple_of(h * 64 + (2 * b + r) * 8, 8), 8)
                    sums[at, c * N : (c + 1) * N] = acc[b][r]

    mixed = move_lanes(sums[...], gather)
    factor = factor_lanes()
    for h in range(GQ):
        for b in range(DP):
            for r in range(2):
                at = h * 64 + (2 * b + r) * 8
                out_ref[b, q * GQ + h, r] = mixed[at : at + 8] * factor


def spread(grad_ref, copy, rep_ref):
    factor = factor_lanes()
    rows = (grad_ref[...] * factor).reshape(DP * CG * 16, N)
    tiles = move_lanes(rows, copy)
    for b in range(DP):
        for g in range(CG):
            for r in range(2):
                at = ((b * CG + g) * 2 + r) * 8
                for c in range(4):
                    rep_ref[4 * g + c, b, r] = tiles[at : at + 8, c * N : (c + 1) * N]


def back_mix(rep_ref, w_ref, i, out_ref):
    def step(t, acc):
        acc = list(acc)
        for u in range(4):
            o = 4 * t + u
            wr, wi = w_ref[0, i, o], w_ref[1, i, o]
            for b in range(DP):
                gr, gi = rep_ref[o, b, 0], rep_ref[o, b, 1]
                acc[2 * b] = acc[2 * b] + (wr * gr + wi * gi)
                acc[2 * b + 1] = acc[2 * b + 1] + (wr * gi - wi * gr)
        return tuple(acc)

    acc = lax.fori_loop(0, 8, step, tuple(jnp.zeros((8, N), F32) for _ in range(8)))
    for b in range(DP):
        for r in range(2):
            out_ref[b, i, r] = acc[2 * b + r]


def weight_grad(rep_ref, spec_ref, o, out_ref):
    grads = [[rep_ref[o, b, r] for r in range(2)] for b in range(DP)]
    for i in range(CG):
        re = im = None
        for b in range(DP):
            gr, gi = grads[b]
            sr, si = spec_ref[b, i, 0], spec_ref[b, i, 1]
            r1 = gr * sr + gi * si
            i1 = gi * sr - gr * si
            re, im = (r1, i1) if b == 0 else (re + r1, im + i1)
        out_ref[0, i, o] = re
        out_ref[1, i, o] = im


def params(collective_id=None):
    if collective_id is None:
        return pltpu.CompilerParams(vmem_limit_bytes=VMEM_LIMIT)
    return pltpu.CompilerParams(
        vmem_limit_bytes=VMEM_LIMIT, collective_id=collective_id, has_side_effects=True
    )


def in_vmem():
    return pl.BlockSpec(memory_space=pltpu.VMEM)


def anywhere():
    return pl.BlockSpec(memory_space=pl.ANY)


def sems(count):
    return pltpu.SemaphoreType.DMA((count,))


SPEC = (DP, CG, 2, 8, N)
FLAT = (M * 64, N)
PIECES = (MP, 64, N)
CELLS = (C, XL, N, N)
PACKED = (2, CG, C, 8, N)


def to_spectrum(flat, pieces, held, out, tx, mp_sems, dp_sems):
    _, mp = position()

    def body(q):
        drain_mp(q, flat, mp_sems[1])
        pieces[mp, piece_rows(q)] = flat[flat_rows(mp, q)]
        forward_x(pieces, q, tx, held)
        send_dp(q, held, out, *dp_sems)
        keep_dp(q, held, out)

    chunks(body)


def plane_copy(src, dst, sem, x):
    return pltpu.make_async_copy(src.at[:, x], dst.at[:, x], sem.at[x])


def move(q, modes, pieces, flat, ix, mp_sems, dp_recv):
    drain_dp(q, modes, dp_recv)
    inverse_x(modes, q, ix, pieces)
    send_to_cells(q, pieces, flat, *mp_sems)


def exchange_mixed(mix_chunk, mixed, modes, dp_sems):
    def body(q):
        mix_chunk(q)
        send_dp(q, mixed, modes, *dp_sems)
        keep_dp(q, mixed, modes)

    chunks(body)


STAGED = 3


def chunk_copy(src, dst, sem, q):
    part = pl.ds(q * 4 * GQ, 4 * GQ)
    return pltpu.make_async_copy(src.at[part], dst.at[part], sem.at[q])


def group_copy(src, dst, sem, g):
    part = pl.ds(4 * g, 4)
    return pltpu.make_async_copy(src.at[part], dst.at[part], sem.at[g])


def layer_kernel(
    field_ref, w_ref, up_ref, pw_ref, bias_ref, ex_ref,
    tz, ty, tx, ix, iy, iz, pack, gather, copy,
    flat_out, wgrad_out, point_out,
    fields, weight, upstream, cells, packed, rep, mat, sums,
    flat1, pieces1, held1, spectrum, mixed2, modes2, pieces2, flat2,
    flat3, pieces3, held3, grad_spec, mixed4, modes4, pieces4, flat4,
    field_sem, weight_sem, up_sem, point_sem,
    m1_send, m1_recv, d1_send, d1_recv, d2_send, d2_recv, m2_send, m2_recv,
    m3_send, m3_recv, d3_send, d3_recv, d4_send, d4_recv, m4_send, m4_recv,
):
    _, mp = position()
    greet()

    @pl.loop(0, STAGED)
    def _(g):
        group_copy(field_ref, fields, field_sem, g).start()

    def transform(g):
        group_copy(field_ref, fields, field_sem, g).wait()

        @pl.when(g < CG - STAGED)
        def _():
            group_copy(field_ref, fields, field_sem, g + STAGED).start()

        forward_group(fields, g, tz, ty, flat1)

    def field_chunk(q):
        groups_of(q, transform)

        @pl.when(q == 0)
        def _():
            await_greetings()

        send_to_modes(q, flat1, pieces1, m1_send, m1_recv)

    chunks(field_chunk)
    weight_copy = pltpu.make_async_copy(w_ref, weight, weight_sem.at[0])
    weight_copy.start()
    up_copy = pltpu.make_async_copy(up_ref, upstream, up_sem.at[0])
    up_copy.start()
    channel_matrix(pw_ref[...].T, ex_ref[...], mat)

    @pl.loop(0, XL)
    def _(x):
        channel_map(fields, x, mat, cells)

    weight_copy.wait()

    @pl.loop(0, CG)
    def _(g):
        for r in range(2):
            tiles = [
                jnp.pad(weight[r, 4 * g + c].reshape(8 * C, M), ((0, 0), (0, N - M)))
                for c in range(4)
            ]
            packed[r, g] = move_lanes(jnp.concatenate(tiles, axis=1), pack).reshape(C, 8, N)

    to_spectrum(flat1, pieces1, held1, spectrum, tx, (m1_send, m1_recv), (d1_send, d1_recv))
    chunks(lambda q: drain_dp(q, spectrum, d1_recv))

    exchange_mixed(
        lambda q: mix(spectrum, packed, q, gather, sums, mixed2), mixed2, modes2, (d2_send, d2_recv)
    )

    def move_on(q):
        move(q, modes2, pieces2, flat2, ix, (m2_send, m2_recv), d2_recv)

    @pl.loop(0, AHEAD)
    def _(q):
        move_on(q)

        @pl.when(q == 0)
        def _():
            drain_mp(0, flat2, m2_send)

    up_copy.wait()

    def cell_group(g):
        spectral = inverse_group(flat2, g, iy, iz)
        for c in range(4):
            cells[4 * g + c] = (
                cells[4 * g + c]
                + spectral[:, c * N : (c + 1) * N].reshape(XL, N, N)
                + bias_ref[4 * g + c]
            )

        @pl.loop(0, 4 * XL)
        def _(t):
            o, x = 4 * g + t // XL, t % XL
            pre = cells[o, x]
            cdf = 0.5 * (1.0 + lax.erf(pre * np.float32(np.sqrt(0.5))))
            density = jnp.exp(-0.5 * pre * pre) * np.float32(1 / np.sqrt(2 * np.pi))
            cells[o, x] = upstream[o, x].astype(F32) * (cdf + pre * density)

        forward_group(cells, g, tz, ty, flat3)

    def cell_chunk(q):
        drain_mp(q, flat2, m2_recv)
        flat2[flat_rows(mp, q)] = pieces2[mp, piece_rows(q)]

        @pl.loop(0, GQ)
        def _(h):
            cell_group(q * GQ + h)

            @pl.when((h == 0) & (q < NQ - AHEAD))
            def _():
                move_on(q + AHEAD)

        send_to_modes(q, flat3, pieces3, m3_send, m3_recv)

    chunks(cell_chunk)
    to_spectrum(flat3, pieces3, held3, grad_spec, tx, (m3_send, m3_recv), (d3_send, d3_recv))
    chunks(lambda q: drain_dp(q, grad_spec, d3_recv))

    spread(grad_spec, copy, rep)
    exchange_mixed(
        lambda q: groups_of(q, lambda i: back_mix(rep, packed, i, mixed4)),
        mixed4, modes4, (d4_send, d4_recv),
    )
    channel_matrix(pw_ref[...], ex_ref[...], mat)
    chunks(lambda q: move(q, modes4, pieces4, flat4, ix, (m4_send, m4_recv), d4_recv))

    @pl.loop(0, XL)
    def _(x):
        channel_map(cells, x, mat, fields)
        plane_copy(fields, point_out, point_sem, x).start()

    @pl.loop(0, C)
    def _(o):
        weight_grad(rep, spectrum, o, wgrad_out)

    def land(q):
        drain_mp(q, flat4, m4_recv)
        flat4[flat_rows(mp, q)] = pieces4[mp, piece_rows(q)]

    chunks(land)
    flat_out[...] = flat4[...]
    for sem in (d1_send, d2_send, d3_send, d4_send):
        chunks(lambda q, sem=sem: drain_dp(q, mixed4, sem))

    for first, sem in ((0, m1_send), (1, m2_send), (0, m3_send), (0, m4_send)):

        @pl.loop(first, NQ)
        def _(q, sem=sem):
            drain_mp(q, flat4, sem)

    @pl.loop(0, XL)
    def _(x):
        plane_copy(fields, point_out, point_sem, x).wait()


def layer(fields, weight, upstream, point_weight, point_bias):
    tabs = [TZ, TY, TX, IX, IY, IZ, PACK, GATHER, COPY]
    return pl.pallas_call(
        layer_kernel,
        in_specs=[anywhere(), anywhere(), anywhere(), in_vmem()]
        + [pl.BlockSpec(memory_space=pltpu.SMEM)]
        + [in_vmem()] * (1 + len(tabs)),
        out_specs=[in_vmem(), in_vmem(), anywhere()],
        out_shape=[
            jax.ShapeDtypeStruct(FLAT, F32),
            jax.ShapeDtypeStruct(PACKED, F32),
            jax.ShapeDtypeStruct(CELLS, F32),
        ],
        scratch_shapes=[
            pltpu.VMEM(CELLS, F32),
            pltpu.VMEM((2, C, C, 8, M), F32),
            pltpu.VMEM(CELLS, BF16),
            pltpu.VMEM(CELLS, F32),
            pltpu.VMEM(PACKED, F32),
            pltpu.VMEM((C, DP, 2, 8, N), F32),
            pltpu.VMEM((16 * C, 8 * C), BF16),
            pltpu.VMEM((GQ * 64, 4 * N), F32),
        ]
        + 2
        * [
            pltpu.VMEM(FLAT, F32),
            pltpu.VMEM(PIECES, F32),
            pltpu.VMEM(SPEC, F32),
            pltpu.VMEM(SPEC, F32),
            pltpu.VMEM(SPEC, F32),
            pltpu.VMEM(SPEC, F32),
            pltpu.VMEM(PIECES, F32),
            pltpu.VMEM(FLAT, F32),
        ]
        + [sems(CG), sems(1), sems(1), sems(XL)]
        + [sems(NQ)] * 16,
        compiler_params=params(1),
    )(
        fields,
        weight,
        upstream,
        point_weight,
        point_bias,
        jnp.asarray(EXPAND),
        *map(jnp.asarray, tabs),
    )


def finish_kernel(flat, point, wgrad, iy, iz, unpack, cells_out, wgrad_out):
    g = pl.program_id(0)
    spectral = inverse_group(flat, g, iy, iz)
    for c in range(4):
        cells_out[c] = point[c] + spectral[:, c * N : (c + 1) * N].reshape(XL, N, N)

    tiles = move_lanes(wgrad[...].reshape(16 * C, N), unpack)
    for r in range(2):
        for c in range(4):
            wgrad_out[r, c] = tiles[
                r * 8 * C : (r + 1) * 8 * C, c * N : c * N + M
            ].reshape(C, 8, M)


def finish(flat, point, wgrad):
    cell_spec = pl.BlockSpec((4, XL, N, N), lambda g: (g, 0, 0, 0))
    return pl.pallas_call(
        finish_kernel,
        grid=(CG,),
        in_specs=[
            whole(FLAT),
            cell_spec,
            pl.BlockSpec((2, pl.Squeezed(), C, 8, N), lambda g: (0, g, 0, 0, 0)),
            whole(IY.shape),
            whole(IZ.shape),
            whole(UNPACK.shape),
        ],
        out_specs=[cell_spec, pl.BlockSpec((2, 4, C, 8, M), lambda g: (0, g, 0, 0, 0))],
        out_shape=[
            jax.ShapeDtypeStruct(CELLS, F32),
            jax.ShapeDtypeStruct((2, C, C, 8, M), F32),
        ],
        compiler_params=params(),
    )(flat, point, wgrad, *map(jnp.asarray, [IY, IZ, UNPACK]))


def shards(fields, upstream, spectral_weight, point_weight, point_bias):
    flat, wgrad, point = layer(
        fields[0], spectral_weight, upstream[0], point_weight, point_bias
    )
    grad_fields, weight_out = finish(flat, point, wgrad)
    return (grad_fields[None], weight_out)


def solution(mesh):
    placed = (
        P("dp", None, "mp", None, None),
        P("dp", None, "mp", None, None),
        P(None, None, None, "dp", "mp"),
        P(),
        P(),
    )
    return jax.shard_map(
        shards,
        mesh=mesh,
        in_specs=placed,
        out_specs=(P("dp", None, "mp", None, None), P(None, None, None, "dp", "mp")),
        check_vma=False,
    )
```

time: 133 us -> 117 us (0.88)
  Pallas kernels: 130 us -> 116 us
  local copies, waits for them, and re-layouts: 1.36 us -> 0 us
    pallas_call x3 -> x1, Pallas kernels: 113 us -> 101 us  [layer(): pl.pallas_call(layer_kernel, in_specs=[anywhere(), anywhere(), anywhere()...]
    pallas_call x1, Pallas kernels: 17.1 us -> 14.5 us  [finish(): pl.pallas_call(finish_kernel, grid=(CG,), in_specs=[whole(FLAT), cell_spe...]
    broadcast_in_dim x1 -> x0, local copies, waits for them, and re-layouts: 1.36 us -> none  [middle(): jnp.broadcast_to(point_bias[:, None, None], (C, 1, N))]
where the time goes in v3:
time: 117 us
  Pallas kernels  116 us (99%)
    pallas_call x1, Pallas kernels, layer(): pl.pallas_call(layer_kernel, in_specs=[anywhere(), anywhere(), anywhere()...  101 us
    pallas_call x1, Pallas kernels, finish(): pl.pallas_call(finish_kernel, grid=(CG,), in_specs=[whole(FLAT), cell_spe...  14.5 us

profile of v3, /device:TPU:1, one launch (start us, length us, event | category | flops | bytes accessed | tf_op | source)
XLA Modules:
  0.0 116.5 jit_solution(4090568169572193424)
XLA Ops:
  0.6 101.4 %shard_map.167 = (f32[2048,128]{1,0:T(8,128)}, f32[2,8,32,8,128]{4,3,2,1,0:T(8,128)}, f32[32,4,128,128]{3,2,1,0:T(8,128)}) custom-call(f32[32,4,128,128]{3,2,1,0:T(8,128)} %bitcast.3, f32[2,32,32,8,32]{4,3,2,1,0:T(8,128)} %w_ref.1, bf16[32,4,128,128]{3,2,1,0:T(8,128)(2,1)} %bitcast.4, f32[32,32]{1,0:T(8,128)} %pw_ref.1, f32[32]{0:T(128)} %bias_ref.1, ...), custom_call_target="tpu_custom_call" | custom-call | tf_op jit(solution)/shard_map/pallas_call | solution.py:665
  102.1 14.5 %shard_map.168 = (f32[32,4,128,128]{3,2,1,0:T(8,128)}, f32[2,32,32,8,32]{4,3,2,1,0:T(8,128)}) custom-call(f32[2048,128]{1,0:T(8,128)} %get-tuple-element.7.flat, f32[32,4,128,128]{3,2,1,0:T(8,128)} %get-tuple-element.8.point, f32[2,8,32,8,128]{4,3,2,1,0:T(8,128)} %get-tuple-element.9.wgrad, bf16[256,192]{1,0:T(8,128)(2,1)} %constant.27.clone.iy, ...), custom_call_target="tpu_custom_call" | custom-call | tf_op jit(solution)/shard_map/pallas_call | solution.py:727

commit v4 on v3

--- a/solution.py
+++ b/solution.py
@@ -134,7 +134,8 @@
 
 
 NQ = 4
-AHEAD = 2
+LEFT = 1
+AHEAD = 4
 GQ = CG // NQ
 RQ = 8 * GQ
 MESH = pl.DeviceIdType.MESH
@@ -476,10 +477,6 @@
     chunks(body)
 
 
-def plane_copy(src, dst, sem, x):
-    return pltpu.make_async_copy(src.at[:, x], dst.at[:, x], sem.at[x])
-
-
 def move(q, modes, pieces, flat, ix, mp_sems, dp_recv):
     drain_dp(q, modes, dp_recv)
     inverse_x(modes, q, ix, pieces)
@@ -506,6 +503,12 @@
 def group_copy(src, dst, sem, g):
     part = pl.ds(4 * g, 4)
     return pltpu.make_async_copy(src.at[part], dst.at[part], sem.at[g])
+
+
+def add_spectral(flat, g, iy, iz, cells):
+    spectral = inverse_group(flat, g, iy, iz)
+    for c in range(4):
+        cells[4 * g + c] = cells[4 * g + c] + spectral[:, c * N : (c + 1) * N].reshape(XL, N, N)
 
 
 def layer_kernel(
@@ -526,7 +529,12 @@
     def _(g):
         group_copy(field_ref, fields, field_sem, g).start()
 
+    def weight_copy(g):
+        part = pl.ds(4 * g, 4)
+        return pltpu.make_async_copy(w_ref.at[:, part], weight.at[:, part], weight_sem.at[g])
+
     def transform(g):
+        weight_copy(g).start()
         group_copy(field_ref, fields, field_sem, g).wait()
 
         @pl.when(g < CG - STAGED)
@@ -545,20 +553,12 @@
         send_to_modes(q, flat1, pieces1, m1_send, m1_recv)
 
     chunks(field_chunk)
-    weight_copy = pltpu.make_async_copy(w_ref, weight, weight_sem.at[0])
-    weight_copy.start()
     up_copy = pltpu.make_async_copy(up_ref, upstream, up_sem.at[0])
     up_copy.start()
     channel_matrix(pw_ref[...].T, ex_ref[...], mat)
-
-    @pl.loop(0, XL)
-    def _(x):
-        channel_map(fields, x, mat, cells)
-
-    weight_copy.wait()
-
     @pl.loop(0, CG)
     def _(g):
+        weight_copy(g).wait()
         for r in range(2):
             tiles = [
                 jnp.pad(weight[r, 4 * g + c].reshape(8 * C, M), ((0, 0), (0, N - M)))
@@ -580,9 +580,9 @@
     def _(q):
         move_on(q)
 
-        @pl.when(q == 0)
-        def _():
-            drain_mp(0, flat2, m2_send)
+    @pl.loop(0, XL)
+    def _(x):
+        channel_map(fields, x, mat, cells)
 
     up_copy.wait()
 
@@ -620,6 +620,7 @@
         send_to_modes(q, flat3, pieces3, m3_send, m3_recv)
 
     chunks(cell_chunk)
+    channel_matrix(pw_ref[...], ex_ref[...], mat)
     to_spectrum(flat3, pieces3, held3, grad_spec, tx, (m3_send, m3_recv), (d3_send, d3_recv))
     chunks(lambda q: drain_dp(q, grad_spec, d3_recv))
 
@@ -628,13 +629,12 @@
         lambda q: groups_of(q, lambda i: back_mix(rep, packed, i, mixed4)),
         mixed4, modes4, (d4_send, d4_recv),
     )
-    channel_matrix(pw_ref[...], ex_ref[...], mat)
-    chunks(lambda q: move(q, modes4, pieces4, flat4, ix, (m4_send, m4_recv), d4_recv))
-
-    @pl.loop(0, XL)
-    def _(x):
-        channel_map(cells, x, mat, fields)
-        plane_copy(fields, point_out, point_sem, x).start()
+
+    def move_back(q):
+        move(q, modes4, pieces4, flat4, ix, (m4_send, m4_recv), d4_recv)
+        channel_map(cells, q, mat, fields)
+
+    chunks(move_back)
 
     @pl.loop(0, C)
     def _(o):
@@ -643,21 +643,25 @@
     def land(q):
         drain_mp(q, flat4, m4_recv)
         flat4[flat_rows(mp, q)] = pieces4[mp, piece_rows(q)]
+
+        @pl.when(q < NQ - LEFT)
+        def _():
+            groups_of(q, lambda g: add_spectral(flat4, g, iy, iz, fields))
+
+        chunk_copy(fields, point_out, point_sem, q).start()
 
     chunks(land)
     flat_out[...] = flat4[...]
     for sem in (d1_send, d2_send, d3_send, d4_send):
         chunks(lambda q, sem=sem: drain_dp(q, mixed4, sem))
 
-    for first, sem in ((0, m1_send), (1, m2_send), (0, m3_send), (0, m4_send)):
+    for first, sem in ((0, m1_send), (0, m2_send), (0, m3_send), (0, m4_send)):
 
         @pl.loop(first, NQ)
         def _(q, sem=sem):
             drain_mp(q, flat4, sem)
 
-    @pl.loop(0, XL)
-    def _(x):
-        plane_copy(fields, point_out, point_sem, x).wait()
+    chunks(lambda q: chunk_copy(fields, point_out, point_sem, q).wait())
 
 
 def layer(fields, weight, upstream, point_weight, point_bias):
@@ -694,7 +698,7 @@
             pltpu.VMEM(PIECES, F32),
             pltpu.VMEM(FLAT, F32),
         ]
-        + [sems(CG), sems(1), sems(1), sems(XL)]
+        + [sems(CG), sems(CG), sems(1), sems(NQ)]
         + [sems(NQ)] * 16,
         compiler_params=params(1),
     )(
@@ -710,9 +714,16 @@
 
 def finish_kernel(flat, point, wgrad, iy, iz, unpack, cells_out, wgrad_out):
     g = pl.program_id(0)
-    spectral = inverse_group(flat, g, iy, iz)
-    for c in range(4):
-        cells_out[c] = point[c] + spectral[:, c * N : (c + 1) * N].reshape(XL, N, N)
+
+    @pl.when(g < CG - LEFT * GQ)
+    def _():
+        cells_out[...] = point[...]
+
+    @pl.when(g >= CG - LEFT * GQ)
+    def _():
+        spectral = inverse_group(flat, g, iy, iz)
+        for c in range(4):
+            cells_out[c] = point[c] + spectral[:, c * N : (c + 1) * N].reshape(XL, N, N)
 
     tiles = move_lanes(wgrad[...].reshape(16 * C, N), unpack)
     for r in range(2):

time: 117 us -> 113 us (0.966)
  Pallas kernels: 116 us -> 113 us
    pallas_call x1, Pallas kernels: 101 us -> 99.3 us  [layer(): pl.pallas_call(layer_kernel, in_specs=[anywhere(), anywhere(), anywhere()...]
    pallas_call x1, Pallas kernels: 14.5 us -> 13.2 us  [finish(): pl.pallas_call(finish_kernel, grid=(CG,), in_specs=[whole(FLAT), cell_spe...]
where the time goes in v4:
time: 113 us
  Pallas kernels  113 us (100%)
    pallas_call x1, Pallas kernels, layer(): pl.pallas_call(layer_kernel, in_specs=[anywhere(), anywhere(), anywhere()...  99.3 us
    pallas_call x1, Pallas kernels, finish(): pl.pallas_call(finish_kernel, grid=(CG,), in_specs=[whole(FLAT), cell_spe...  13.2 us

profile of v4, /device:TPU:1, one launch (start us, length us, event | category | flops | bytes accessed | tf_op | source)
XLA Modules:
  0.0 113.2 jit_solution(7655354826709172363)
XLA Ops:
  0.6 99.3 %shard_map.167 = (f32[2048,128]{1,0:T(8,128)}, f32[2,8,32,8,128]{4,3,2,1,0:T(8,128)}, f32[32,4,128,128]{3,2,1,0:T(8,128)}) custom-call(f32[32,4,128,128]{3,2,1,0:T(8,128)} %bitcast.3, f32[2,32,32,8,32]{4,3,2,1,0:T(8,128)} %w_ref.1, bf16[32,4,128,128]{3,2,1,0:T(8,128)(2,1)} %bitcast.4, f32[32,32]{1,0:T(8,128)} %pw_ref.1, f32[32]{0:T(128)} %bias_ref.1, ...), custom_call_target="tpu_custom_call" | custom-call | tf_op jit(solution)/shard_map/pallas_call | solution.py:669
  100.0 13.2 %shard_map.168 = (f32[32,4,128,128]{3,2,1,0:T(8,128)}, f32[2,32,32,8,32]{4,3,2,1,0:T(8,128)}) custom-call(f32[2048,128]{1,0:T(8,128)} %get-tuple-element.7.flat, f32[32,4,128,128]{3,2,1,0:T(8,128)} %get-tuple-element.8.point, f32[2,8,32,8,128]{4,3,2,1,0:T(8,128)} %get-tuple-element.9.wgrad, bf16[256,192]{1,0:T(8,128)(2,1)} %constant.27.clone.iy, ...), custom_call_target="tpu_custom_call" | custom-call | tf_op jit(solution)/shard_map/pallas_call | solution.py:738

commit v5 on v4

--- a/solution.py
+++ b/solution.py
@@ -630,15 +630,18 @@
         mixed4, modes4, (d4_send, d4_recv),
     )
 
-    def move_back(q):
-        move(q, modes4, pieces4, flat4, ix, (m4_send, m4_recv), d4_recv)
-        channel_map(cells, q, mat, fields)
-
-    chunks(move_back)
-
     @pl.loop(0, C)
     def _(o):
         weight_grad(rep, spectrum, o, wgrad_out)
+
+    def move_back(q):
+        move(q, modes4, pieces4, flat4, ix, (m4_send, m4_recv), d4_recv)
+
+    chunks(move_back)
+
+    @pl.loop(0, XL)
+    def _(x):
+        channel_map(cells, x, mat, fields)
 
     def land(q):
         drain_mp(q, flat4, m4_recv)

time: 113 us -> 113 us (level)
  no operation moved by 1% of the time
where the time goes in v5:
time: 113 us
  Pallas kernels  112 us (99%)
    pallas_call x1, Pallas kernels, layer(): pl.pallas_call(layer_kernel, in_specs=[anywhere(), anywhere(), anywhere()...  99.2 us
    pallas_call x1, Pallas kernels, finish(): pl.pallas_call(finish_kernel, grid=(CG,), in_specs=[whole(FLAT), cell_spe...  13.2 us

profile of v5, /device:TPU:1, one launch (start us, length us, event | category | flops | bytes accessed | tf_op | source)
XLA Modules:
  0.0 113.1 jit_solution(2519725286683911041)
XLA Ops:
  0.6 99.2 %shard_map.167 = (f32[2048,128]{1,0:T(8,128)}, f32[2,8,32,8,128]{4,3,2,1,0:T(8,128)}, f32[32,4,128,128]{3,2,1,0:T(8,128)}) custom-call(f32[32,4,128,128]{3,2,1,0:T(8,128)} %bitcast.3, f32[2,32,32,8,32]{4,3,2,1,0:T(8,128)} %w_ref.1, bf16[32,4,128,128]{3,2,1,0:T(8,128)(2,1)} %bitcast.4, f32[32,32]{1,0:T(8,128)} %pw_ref.1, f32[32]{0:T(128)} %bias_ref.1, ...), custom_call_target="tpu_custom_call" | custom-call | tf_op jit(solution)/shard_map/pallas_call | solution.py:672
  99.9 13.2 %shard_map.168 = (f32[32,4,128,128]{3,2,1,0:T(8,128)}, f32[2,32,32,8,32]{4,3,2,1,0:T(8,128)}) custom-call(f32[2048,128]{1,0:T(8,128)} %get-tuple-element.7.flat, f32[32,4,128,128]{3,2,1,0:T(8,128)} %get-tuple-element.8.point, f32[2,8,32,8,128]{4,3,2,1,0:T(8,128)} %get-tuple-element.9.wgrad, bf16[256,192]{1,0:T(8,128)(2,1)} %constant.27.clone.iy, ...), custom_call_target="tpu_custom_call" | custom-call | tf_op jit(solution)/shard_map/pallas_call | solution.py:741
